TPU v7x, 512 devices: a whole 4x4x16 slice. The times are simulated.
512 devices in a mesh: gy: 128 (over y, x, z_lo, core), gz: 4 (over z_hi).
Axes of the slice: x: 4, y: 4, z: 16 (z_hi: 4, z_lo: 4; z = z_hi * 4 + z_lo), core: 2. Of those that a mesh axis runs over, the one named last changes fastest.
Arguments:
- volume: float32 [160, 128, 4096], P('gz', 'gy'), may hold values from -6 to 6
- x_offsets: int32 [160], replicated, may hold values from -64 to 64, as said below
- x_fracs: float32 [160], replicated, may hold values from 0 to 1
- z_offsets: int32 [128], P('gy'), may hold values from -4 to 4, as said below
- z_fracs: float32 [128], P('gy'), may hold values from 0 to 1
- y_offsets: int32 [4096], P('gy'), may hold values from -32 to 32, as said below
- y_fracs: float32 [4096], P('gy'), may hold values from 0 to 1
- slopes: int32 [8], replicated, may hold values from -4 to 4, as said below
Outputs:
- rotated: float32 [160, 128, 4096], P('gz', 'gy')
- projections: float32 [8, 4096, 128], P('gz', 'gy')
Inputs may be any that keep to these rules, and one draw needn't show every extreme that they name: `x_offsets`: each value between -64 and 64, both ends taken by some plane. `z_offsets`: each value between -4 and 4, both ends taken by some row. `y_offsets`: each value between -32 and 32, both ends taken by some column. `slopes`: each value between -4 and 4, both ends taken by some tilt.
All inputs are finite; a program needn't handle non-finite values.
Results may differ from a plain program's by a relative error of at most 0.0003.
Values sent between devices are 32-bit elements; how exact they have to be, the bound alone decides.
A program may use at most 64 MiB of HBM per device.

v0:
```python
import jax
import jax.numpy as jnp
from jax import lax
from jax.sharding import PartitionSpec as P

TAPS = 64
OFFX = 64
OFFZ = 4


def with_halo(value, sides, width):
    for axis, dim in sides:
        peers, length = (lax.axis_size(axis), value.shape[dim])
        up = [(i, (i + 1) % peers) for i in range(peers - 1)]
        down = [(j, i) for i, j in up]
        last = lax.slice_in_dim(value, length - width, length, axis=dim)
        first = lax.slice_in_dim(value, 0, width, axis=dim)
        before = lax.ppermute(last, axis, up)
        after = lax.ppermute(first, axis, down)
        value = jnp.concatenate([before, value, after], axis=dim)
    return value


def tap_weight(offset, fraction):
    moved = offset.astype(jnp.float32) - fraction
    inside = (offset >= 1 - TAPS // 2) & (offset <= TAPS // 2)
    value = jnp.sinc(moved) * (0.5 + 0.5 * jnp.cos(jnp.pi * moved / (TAPS // 2 + 1)))
    return jnp.where(inside, value, jnp.zeros_like(value))


def shear_lines(planes, shifts, fractions):
    plane_total, row_total, line_length = planes.shape
    tile_width = 128
    margin = OFFX + tile_width
    padded = jnp.pad(planes, ((0, 0), (0, 0), (margin, margin)))
    starts = margin + shifts - (TAPS // 2 - 1)
    spans = jax.vmap(
        lambda one_plane, first_index: lax.dynamic_slice_in_dim(
            one_plane, first_index, line_length + tile_width, 1
        )
    )(padded, starts)
    tile_count = line_length // tile_width
    pieces = spans.reshape(plane_total, row_total, tile_count + 1, tile_width)
    windows = jnp.concatenate([pieces[:, :, :-1], pieces[:, :, 1:]], axis=3)
    inner_index = jnp.arange(2 * tile_width, dtype=jnp.int32)[:, None]
    outer_index = jnp.arange(tile_width, dtype=jnp.int32)[None, :]
    band_matrix = tap_weight(
        (inner_index - outer_index - (TAPS // 2 - 1))[None], fractions[:, None, None]
    )
    sheared = jnp.einsum("prbj,pji->prbi", windows, band_matrix, precision=lax.Precision.HIGHEST)
    return sheared.reshape(plane_total, row_total, line_length)


def local(volume, x_offsets, x_fracs, z_offsets, z_fracs, y_offsets, y_fracs, slopes):
    depth = TAPS // 2 + OFFZ
    plane_count, row_local, width_all = volume.shape
    groups = lax.axis_size("gy")
    col_local = width_all // groups
    first_plane = lax.axis_index("gz") * plane_count
    plane_shifts = lax.dynamic_slice_in_dim(x_offsets, first_plane, plane_count)
    plane_fracs = lax.dynamic_slice_in_dim(x_fracs, first_plane, plane_count)
    sheared_x = shear_lines(volume, plane_shifts, plane_fracs)
    extended = with_halo(sheared_x, (("gz", 0),), depth)
    plane_index = jnp.arange(plane_count, dtype=jnp.int32)[:, None]
    source_index = jnp.arange(plane_count + 2 * depth, dtype=jnp.int32)[None, :]
    mixing = tap_weight(
        (source_index - depth - plane_index)[None] - z_offsets[:, None, None],
        z_fracs[:, None, None],
    )
    blocked = extended.reshape(plane_count + 2 * depth, row_local, groups, col_local)
    outgoing = jnp.einsum("rzj,jrgc->grcz", mixing, blocked, precision=lax.Precision.HIGHEST)
    outgoing = outgoing.reshape(groups, 1, row_local * col_local * plane_count)
    arrived = lax.all_to_all(outgoing, "gy", split_axis=0, concat_axis=1, tiled=True)
    row_total = groups * row_local
    columns = arrived.reshape(row_total, col_local, plane_count)
    target_row = jnp.arange(row_total, dtype=jnp.int32)[:, None]
    source_row = jnp.arange(row_total, dtype=jnp.int32)[None, :]
    operator = tap_weight(
        (source_row - target_row)[None] - y_offsets[:, None, None], y_fracs[:, None, None]
    )
    rotated_cols = jnp.einsum("cij,jcz->zci", operator, columns, precision=lax.Precision.HIGHEST)
    span_pad = row_total // 4
    total_planes = plane_count * lax.axis_size("gz")
    global_planes = first_plane + jnp.arange(plane_count, dtype=jnp.int32)
    padded_cols = jnp.pad(rotated_cols, ((0, 0), (0, 0), (span_pad, span_pad)))
    per_tilt = []
    for tilt_index in range(slopes.shape[0]):
        lifts = (
            slopes[tilt_index]
            * (2 * global_planes - total_planes)
            * row_total
            // (16 * total_planes)
        )
        moved = jax.vmap(
            lambda one_plane, lift_one: lax.dynamic_slice_in_dim(
                one_plane, span_pad + lift_one, row_total, 1
            )
        )(padded_cols, lifts)
        per_tilt.append(jnp.sum(moved, axis=0))
    partial_terms = jnp.stack(per_tilt) * total_planes ** (-0.5)
    projections = lax.psum_scatter(partial_terms, "gz", scatter_dimension=0, tiled=True)
    returning = rotated_cols.reshape(plane_count, col_local, groups, row_local)
    returning = jnp.transpose(returning, (2, 3, 1, 0)).reshape(
        groups, 1, row_local * col_local * plane_count
    )
    landed = lax.all_to_all(returning, "gy", split_axis=0, concat_axis=1, tiled=True)
    landed = landed.reshape(groups, row_local, col_local, plane_count)
    rotated = jnp.transpose(landed, (3, 1, 0, 2)).reshape(
        plane_count, row_local, groups * col_local
    )
    return (rotated, projections)


def solution(mesh):
    return jax.shard_map(
        local,
        mesh=mesh,
        in_specs=(P("gz", "gy", None), P(), P(), P("gy"), P("gy"), P("gy"), P("gy"), P()),
        out_specs=(P("gz", "gy", None), P("gz", "gy", None)),
        check_vma=False,
    )
```

profile of v0, /device:TPU:25, one launch (start us, length us, event | category | flops | bytes accessed | tf_op | source)
XLA Modules:
  0.0 374.3 jit_solution(456405718295393765)
XLA Ops:
  8.8 2.5 pad.17
  11.3 85.5 %while.1 = (s32[]{:T(128)}, f32[40,1,4480]{2,1,0:T(1,128)S(1)}, s32[40,3]{0,1:T(4,128)S(1)}, f32[40,1,4224]{2,1,0:T(1,128)S(1)}, s32[]{:T(128)}) while((s32[]{:T(128)}, f32[40,1,4480]{2,1,0:T(1,128)S(1)}, s32[40,3]{0,1:T(4,128)S(1)}, f32[40,1,4224]{2,1,0:T(1,128)S(1)}, s32[]{:T(128)}) %tuple.40), condition=%wide.while_cond, body=%wide.while_body.sunk | while | flops 2 | bytes 33917 | solution.py:38
  98.7 27.8 %fusion.28 = f32[40,32,128]{2,1,0:T(8,128)S(1)} fusion(f32[40]{0:T(128)S(1)} %dynamic_slice.7, f32[256,128]{1,0:T(8,128)S(1)} %fusion.107, pred[256,128]{1,0:T(8,128)(4,1)S(1)} %fusion.110, f32[40,1,32,128]{3,2,0,1:T(8,128)S(1)} %get-tuple-element.29, f32[40,1,32,128]{3,2,0,1:T(8,128)S(1)} %get-tuple-element.28), kind=kOutput, calls=%fused_computation.46 | convolution fusion | flops 554762240 | bytes 2130080 | tf_op jit(solution)/shard_map/prbj,pji->prbi/dot_general | solution.py:50
  127.7 9.6 %collective-permute-start = (f32[36,1,4096]{2,1,0:T(1,128)}, f32[36,1,4096]{2,1,0:T(1,128)}, u32[]{:S(2)}, u32[]{:S(2)}) collective-permute-start(f32[36,1,4096]{2,1,0:T(1,128)} %bitcast.2), channel_id=1, source_target_pairs={{0,1},{1,2},{2,3},{4,5},{5,6},{6,7},{8,9},{9,10},{10,11},{12,13},{... | collective-permute-start | bytes 1769480 | tf_op jit(solution)/shard_map/ppermute | solution.py:18
  142.3 6.6 %collective-permute-done = f32[36,1,4096]{2,1,0:T(1,128)} collective-permute-done((f32[36,1,4096]{2,1,0:T(1,128)}, f32[36,1,4096]{2,1,0:T(1,128)}, u32[]{:S(2)}, u32[]{:S(2)}) %collective-permute-start) | collective-permute-done | bytes 589856 | tf_op jit(solution)/shard_map/ppermute | solution.py:18
  148.9 2.5 reduce.1
  153.7 43.0 %collective-permute-done.1 = f32[36,1,4096]{2,1,0:T(1,128)} collective-permute-done((f32[36,1,4096]{2,1,0:T(1,128)}, f32[36,1,4096]{2,1,0:T(1,128)}, u32[]{:S(2)}, u32[]{:S(2)}) %collective-permute-start.1) | collective-permute-done | bytes 589856 | tf_op jit(solution)/shard_map/ppermute | solution.py:19
  196.7 2.5 reduce.2
  201.5 2.6 fusion.83
  205.3 9.7 %all-to-all-start = ((f32[128,1,1280]{2,1,0:T(1,128)}), f32[128,1,1280]{2,1,0:T(1,128)S(1)}, u32[]{:S(2)}, u32[]{:S(2)}) async-start(f32[128,1,1280]{2,1,0:T(1,128)} %copy.70), calls=%async_computation | async-start | bytes 1310720 | tf_op jit(solution)/shard_map/all_to_all | solution.py:73
  215.1 18.2 %all-to-all-done = f32[128,1,1280]{2,1,0:T(1,128)S(1)} async-done(((f32[128,1,1280]{2,1,0:T(1,128)}), f32[128,1,1280]{2,1,0:T(1,128)S(1)}, u32[]{:S(2)}, u32[]{:S(2)}) %all-to-all-start) | async-done | bytes 655392 | tf_op jit(solution)/shard_map/all_to_all | solution.py:73
  234.2 13.8 %fusion.77 = f32[32,40,128]{2,1,0:T(8,128)S(1)} fusion(f32[128,32,40]{0,2,1:T(8,128)S(1)} %bitcast.76, f32[32]{0:T(128)S(1)} %copy-done.3, s32[32]{0:T(128)S(1)} %copy-done.4, s32[128,128]{1,0:T(8,128)S(1)} %iota_subtract_fusion), kind=kOutput, calls=%fused_computation.100 | convolution fusion | flops 274726912 | bytes 1376512 | tf_op jit(solution)/shard_map/cij,jcz->zci/dot_general | solution.py:81
  249.1 9.6 %all-to-all-start.1 = ((f32[128,1,1280]{2,1,0:T(1,128)}), f32[128,1,1280]{2,1,0:T(1,128)S(1)}, u32[]{:S(2)}, u32[]{:S(2)}) async-start(f32[128,1,1280]{2,1,0:T(1,128)} %copy.72), calls=%async_computation.1 | async-start | bytes 1310720 | tf_op jit(solution)/shard_map/all_to_all | solution.py:106
  264.6 2.2 copy.92
  266.8 2.1 pad.18.clone
  268.9 7.5 %gather_fusion.7 = f32[40,32,128]{1,0,2:T(8,128)S(1)} fusion(f32[40,32,192]{1,0,2:T(8,128)} %pad.18.clone, s32[40]{0:T(128)S(1)} %get-tuple-element.40), kind=kCustom, calls=%fused_computation.7 | custom fusion | bytes 1311200 | tf_op jit(solution)/shard_map/vmap()/gather | solution.py:95
  276.9 7.5 %gather_fusion.6 = f32[40,32,128]{1,0,2:T(8,128)S(1)} fusion(f32[40,32,192]{1,0,2:T(8,128)} %pad.18.clone, s32[40]{0:T(128)S(1)} %get-tuple-element.41), kind=kCustom, calls=%fused_computation.6 | custom fusion | bytes 1311200 | tf_op jit(solution)/shard_map/vmap()/gather | solution.py:95
  284.9 7.5 %gather_fusion.5 = f32[40,32,128]{1,0,2:T(8,128)S(1)} fusion(f32[40,32,192]{1,0,2:T(8,128)} %pad.18.clone, s32[40]{0:T(128)S(1)} %get-tuple-element.42), kind=kCustom, calls=%fused_computation.5 | custom fusion | bytes 1311200 | tf_op jit(solution)/shard_map/vmap()/gather | solution.py:95
  292.9 8.3 %gather_fusion.4 = f32[40,32,128]{1,0,2:T(8,128)S(1)} fusion(f32[40,32,192]{1,0,2:T(8,128)} %pad.18.clone, s32[40]{0:T(128)S(1)} %get-tuple-element.43), kind=kCustom, calls=%fused_computation.4 | custom fusion | bytes 1311200 | tf_op jit(solution)/shard_map/vmap()/gather | solution.py:95
  301.6 8.6 %gather_fusion.3 = f32[40,32,128]{1,0,2:T(8,128)S(1)} fusion(f32[40,32,192]{1,0,2:T(8,128)} %pad.18.clone, s32[40]{0:T(128)S(1)} %get-tuple-element.44), kind=kCustom, calls=%fused_computation.3 | custom fusion | bytes 1311200 | tf_op jit(solution)/shard_map/vmap()/gather | solution.py:95
  310.6 7.5 %gather_fusion.2 = f32[40,32,128]{1,0,2:T(8,128)S(1)} fusion(f32[40,32,192]{1,0,2:T(8,128)} %pad.18.clone, s32[40]{0:T(128)S(1)} %get-tuple-element.45), kind=kCustom, calls=%fused_computation.2 | custom fusion | bytes 1311200 | tf_op jit(solution)/shard_map/vmap()/gather | solution.py:95
  318.6 7.5 %gather_fusion.1 = f32[40,32,128]{1,0,2:T(8,128)S(1)} fusion(f32[40,32,192]{1,0,2:T(8,128)} %pad.18.clone, s32[40]{0:T(128)S(1)} %get-tuple-element.46), kind=kCustom, calls=%fused_computation.1 | custom fusion | bytes 1311200 | tf_op jit(solution)/shard_map/vmap()/gather | solution.py:95
  326.5 7.5 %gather_fusion = f32[40,32,128]{1,0,2:T(8,128)S(1)} fusion(f32[40,32,192]{1,0,2:T(8,128)} %pad.18.clone, s32[40]{0:T(128)S(1)} %get-tuple-element.47), kind=kCustom, calls=%fused_computation | custom fusion | bytes 1311200 | tf_op jit(solution)/shard_map/vmap()/gather | solution.py:95
  339.0 28.2 %reduce-scatter.2.cloned.1.call-done = f32[2,32,128]{2,1,0:T(8,128)} async-done(((f32[8,32,128]{2,1,0:T(8,128)}), f32[2,32,128]{2,1,0:T(8,128)}) %reduce-scatter.2.cloned.1.call-update) | async-done | bytes 32784 | tf_op jit(solution)/shard_map/reduce_scatter | solution.py:101
  (189 shorter events, 114.6 us)
Async XLA Ops:
  127.7 21.2 %collective-permute-start = (f32[36,1,4096]{2,1,0:T(1,128)}, f32[36,1,4096]{2,1,0:T(1,128)}, u32[]{:S(2)}, u32[]{:S(2)}) collective-permute-start(f32[36,1,4096]{2,1,0:T(1,128)} %bitcast.2), channel_id=1, source_target_pairs={{0,1},{1,2},{2,3},{4,5},{5,6},{6,7},{8,9},{9,10},{10,11},{12,13},{... | collective-permute-start | bytes 1769480 | tf_op jit(solution)/shard_map/ppermute | solution.py:18
  137.3 59.4 %collective-permute-start.1 = (f32[36,1,4096]{2,1,0:T(1,128)}, f32[36,1,4096]{2,1,0:T(1,128)}, u32[]{:S(2)}, u32[]{:S(2)}) collective-permute-start(f32[36,1,4096]{2,1,0:T(1,128)} %bitcast.3), channel_id=1, source_target_pairs={{1,0},{2,1},{3,2},{5,4},{6,5},{7,6},{9,8},{10,9},{11,10},{13,12},{... | collective-permute-start | bytes 1769480 | tf_op jit(solution)/shard_map/ppermute | solution.py:19
  199.9 1.6 copy-start.1
  204.1 30.0 %copy-start.3 = (f32[32]{0:T(128)S(1)}, f32[32]{0:T(128)}, u32[]{:S(2)}) copy-start(f32[32]{0:T(128)} %param.14) | copy-start | bytes 388
  204.2 30.0 %copy-start.4 = (s32[32]{0:T(128)S(1)}, s32[32]{0:T(128)}, u32[]{:S(2)}) copy-start(s32[32]{0:T(128)} %param.13) | copy-start | bytes 388
  205.3 28.0 %all-to-all-start = ((f32[128,1,1280]{2,1,0:T(1,128)}), f32[128,1,1280]{2,1,0:T(1,128)S(1)}, u32[]{:S(2)}, u32[]{:S(2)}) async-start(f32[128,1,1280]{2,1,0:T(1,128)} %copy.70), calls=%async_computation | async-start | bytes 1310720 | tf_op jit(solution)/shard_map/all_to_all | solution.py:73
  247.9 16.6 %copy-start = (f32[32,40,128]{2,1,0:T(8,128)}, f32[32,40,128]{2,1,0:T(8,128)S(1)}, u32[]{:S(2)}) copy-start(f32[32,40,128]{2,1,0:T(8,128)S(1)} %fusion.77) | copy-start | bytes 1966084
  247.9 10.8 %copy-start.2 = (s32[8]{0:T(128)S(1)}, s32[8]{0:T(128)}, u32[]{:S(2)}) copy-start(s32[8]{0:T(128)} %param.15) | copy-start | bytes 100
  249.1 86.2 %all-to-all-start.1 = ((f32[128,1,1280]{2,1,0:T(1,128)}), f32[128,1,1280]{2,1,0:T(1,128)S(1)}, u32[]{:S(2)}, u32[]{:S(2)}) async-start(f32[128,1,1280]{2,1,0:T(1,128)} %copy.72), calls=%async_computation.1 | async-start | bytes 1310720 | tf_op jit(solution)/shard_map/all_to_all | solution.py:106
  258.7 108.5 %reduce-scatter.2.cloned.1.call-start = ((), (), s32[]{:S(2)}) async-start(), calls=%async_computation.3 | async-start | bytes 163840 | tf_op jit(solution)/shard_map/reduce_scatter | solution.py:101
Sparse Core Ops, SparseCore 0:
  335.4 31.8 reduce-scatter.1
where the time goes:
time: 382 us; the launch traced here: 374 us
  local copies, waits for them, and re-layouts  171 us (45%)
  waiting for transfers between devices  96 us (25%)
  matrix products  44.2 us (12%)
  starting transfers between devices  30.3 us (8%)
  other arithmetic  16.3 us (4%)
  between operations  16 us (4%)
    gather x120, local copies, waits for them, and re-layouts  84.8 us
    gather x8, local copies, waits for them, and re-layouts, local(): lax.dynamic_slice_in_dim(one_plane, span_pad + lift_one, row_total, 1)  61.9 us
    ppermute x1, waiting for transfers between devices, with_halo(): after = lax.ppermute(first, axis, down)  43 us
    reduce_scatter x1, waiting for transfers between devices, local(): lax.psum_scatter(partial_terms, 'gz', scatter_dimension=0, tiled=True)  28.2 us
    dot_general x1, matrix products, shear_lines(): jnp.einsum('prbj,pji->prbi', windows, band_matrix, precision=lax.Precisio...  27.8 us
    all_to_all x1, waiting for transfers between devices, local(): lax.all_to_all(outgoing, 'gy', split_axis=0, concat_axis=1, tiled=True)  18.2 us
    dot_general x1, matrix products, local(): jnp.einsum('cij,jcz->zci', operator, columns, precision=lax.Precision.HIG...  13.8 us
    all_to_all x1, starting transfers between devices, local(): lax.all_to_all(outgoing, 'gy', split_axis=0, concat_axis=1, tiled=True)  9.74 us
  transfers between devices with their start and end apart: 5, of which 4 were waited for; matrix products, arithmetic and copies ran while one was open for 23% of the time, Pallas kernels for 0%

commit v1 on v0

v1 whole, which is shorter than its diff:
```python
import functools

import jax
import jax.numpy as jnp
from jax import lax
from jax.experimental import pallas as pl
from jax.experimental.pallas import tpu as pltpu
from jax.sharding import PartitionSpec as P

TAPS = 64
ROWS = 32
PLANES = 40
DEPTH = 160
PLACES = 16
TILTS = 8
SLOPE = 4
F32 = jnp.float32
BF16 = jnp.bfloat16
VMEM_BYTES = 48 * 1024 * 1024


def tap_weight(offset, fraction):
    moved = offset.astype(F32) - fraction
    inside = (offset >= 1 - TAPS // 2) & (offset <= TAPS // 2)
    angle = jnp.pi * moved
    centre = moved == 0.0
    ratio = jnp.sin(angle) / jnp.where(centre, 1.0, angle)
    sinc = jnp.where(centre, 1.0, ratio)
    value = sinc * (0.5 + 0.5 * jnp.cos(jnp.pi * moved / (TAPS // 2 + 1)))
    return jnp.where(inside, value, 0.0)


def halves(value):
    high = value.astype(BF16)
    return high, (value - high.astype(F32)).astype(BF16)


def product(left, right):
    left_high, left_low = left
    right_high, right_low = right
    dot = functools.partial(jnp.dot, preferred_element_type=F32)
    return dot(left_high, right_high) + (dot(left_low, right_high) + dot(left_high, right_low))


def iota(shape, axis):
    return lax.broadcasted_iota(jnp.int32, shape, axis)


def band(row, rows):
    wide = jnp.broadcast_to(row, (rows, row.shape[1]))
    return pltpu.roll(wide, 0, 1, stride=1, stride_axis=0)


def shear_x(offs, fracs, y_offs, y_fracs, z_off, z_frac, planes, out, params, taps):
    first = lax.axis_index("gz") * PLANES
    sub = iota((8, 128), 0)
    for block in range(PLANES // 8):
        off = jnp.zeros((8, 128), jnp.int32)
        frac = jnp.zeros((8, 128), F32)
        for s in range(8):
            off = jnp.where(sub == s, offs[first + 8 * block + s], off)
            frac = jnp.where(sub == s, fracs[first + 8 * block + s], frac)
        for part in range(2):
            lane = iota((8, 128), 1) + 128 * part
            weights = tap_weight(128 - lane - off, frac)
            taps[8 * block : 8 * block + 8, 128 * part : 128 * part + 128] = weights
        taps[8 * block : 8 * block + 8, 256:384] = jnp.zeros((8, 128), F32)
    row = iota((ROWS, 128), 0)

    def plane(z, carry):
        matrix = band(taps[pl.ds(z, 1), :], 128)
        total = product(halves(planes[z]), halves(matrix))
        after = jnp.where(row < ROWS - 1, pltpu.roll(total[:, :128], ROWS - 1, 0), 0.0)
        before = jnp.where(row > 0, pltpu.roll(total[:, 256:], 1, 0), 0.0)
        out[pl.ds(z, ROWS, stride=PLANES), :] = total[:, 128:256] + (after + before)
        return carry

    lax.fori_loop(0, PLANES, plane, 0, unroll=4)
    params[...] = jnp.zeros((8, 128), F32)
    params[0:1, 0:32] = y_offs[...].astype(F32)
    params[1:2, 0:32] = y_fracs[...]
    params[2:3, :] = jnp.full((1, 128), z_off[0], jnp.int32).astype(F32)
    params[3:4, :] = jnp.full((1, 128), z_frac[0], F32)


def shear_z(lines, params, out, taps, mixed):
    lane = iota((8, 256), 1)
    target = jnp.where(lane < DEPTH, lane, lane - 256)
    off = params[:, 2, :][:, 0:1].astype(jnp.int32)
    frac = params[:, 3, :][:, 0:1]
    taps[...] = tap_weight(target - off, frac)

    for q in range(8):
        matrix = band(taps[q : q + 1, :], DEPTH)[:, :DEPTH]
        value = product(halves(matrix), halves(lines[q]))
        mixed[pl.ds(q, DEPTH, stride=8), :] = value
    for block in range(10):
        turned = mixed[128 * block : 128 * block + 128, :].T
        out[:, block] = turned.reshape(PLACES, 8, 128)


def exchange(values):
    group = iota((8, 128), 1) // 8
    values = list(values)
    for step in (1, 2, 4, 8):
        keep = (group // step) % 2 == 0
        for low in range(16):
            if low & step == 0:
                a, b = values[low], values[low | step]
                values[low] = jnp.where(keep, a, pltpu.roll(b, 8 * step, 1))
                values[low | step] = jnp.where(keep, pltpu.roll(a, 128 - 8 * step, 1), b)
    return values


def shear_y(slopes, blocks, params, out, projections, taps, before, after, table):
    def unpack(q, carry):
        values = exchange([blocks[p, q] for p in range(16)])
        for z in range(16):
            before[pl.ds(pl.multiple_of(128 * q + 8 * z, 8), 8), :] = values[z]
        return carry

    lax.fori_loop(0, 10, unpack, 0)
    start = 8 * (lax.axis_index("gy") // 8 % 4)
    pick = iota((8, 128), 1) == start + iota((8, 128), 0)
    off = jnp.sum(jnp.where(pick, params[0:1, :], 0.0), axis=1, keepdims=True)
    frac = jnp.sum(jnp.where(pick, params[1:2, :], 0.0), axis=1, keepdims=True)
    lane = iota((8, 256), 1)
    target = jnp.where(lane < 128, lane, lane - 256)
    taps[...] = tap_weight(-target - off.astype(jnp.int32), frac)

    for x in range(8):
        matrix = band(taps[x : x + 1, :], 128)[:, :128]
        value = product(halves(before[pl.ds(x, DEPTH, stride=8), :]), halves(matrix))
        after[pl.ds(x, DEPTH, stride=8), :] = value

    lane = iota((8, 128), 1)
    zero = jnp.zeros((8, 128), F32)
    count = 2 * SLOPE + 1
    sums, totals = [zero] * count, [zero] * count
    for z in range(DEPTH):
        value = after[8 * z : 8 * z + 8, :]
        for i in range(count):
            lift = (i - SLOPE) * (2 * z - DEPTH) * 128 // (16 * DEPTH)
            following = (i - SLOPE) * (2 * z + 2 - DEPTH) * 128 // (16 * DEPTH)
            sums[i] = sums[i] + value
            if z == DEPTH - 1 or lift != following:
                moved = sums[i]
                if lift > 0:
                    moved = jnp.where(lane < 128 - lift, pltpu.roll(moved, 128 - lift, 1), 0.0)
                elif lift < 0:
                    moved = jnp.where(lane >= -lift, pltpu.roll(moved, -lift, 1), 0.0)
                totals[i] = totals[i] + moved
                sums[i] = zero
    for i in range(count):
        table[i] = totals[i] * DEPTH ** (-0.5)
    for t in range(TILTS):
        projections[t] = table[slopes[t] + SLOPE]

    def pack(q, carry):
        rows = [after[pl.ds(pl.multiple_of(128 * q + 8 * z, 8), 8), :] for z in range(16)]
        values = exchange(rows)
        for p in range(16):
            out[p, q] = values[p]
        return carry

    lax.fori_loop(0, 10, pack, 0)


def turn_back(blocks, out):
    for block in range(10):
        turned = blocks[:, block].reshape(128, 128).T
        for z in range(16):
            out[pl.ds(16 * block + z, 8, stride=DEPTH), :] = turned[8 * z : 8 * z + 8, :]


def restore(lines, out):
    for z in range(PLANES):
        out[z] = lines[pl.ds(z, ROWS, stride=PLANES), :]


def compute(body, outs, scratch, operands, spaces, **cost):
    return pl.pallas_call(
        body,
        out_shape=outs,
        in_specs=[pl.BlockSpec(memory_space=space) for space in spaces],
        scratch_shapes=scratch,
        compiler_params=pltpu.CompilerParams(vmem_limit_bytes=VMEM_BYTES),
    )(*operands)


def position():
    g, j = lax.axis_index("gz"), lax.axis_index("gy")
    return g, j, j // 8, j % 8, g * 8 + j % 8


def copy_to(src, dst, send, recv, g, j):
    return pltpu.make_async_remote_copy(
        src_ref=src,
        dst_ref=dst,
        send_sem=send,
        recv_sem=recv,
        device_id={"gz": g, "gy": j},
        device_id_type=pl.DeviceIdType.MESH,
    )


def signal(g, j):
    pl.semaphore_signal(
        pltpu.get_barrier_semaphore(),
        inc=1,
        device_id={"gz": g, "gy": j},
        device_id_type=pl.DeviceIdType.MESH,
    )


def send_z(lines, params, out, z_params, y_params, send, recv, z_send, z_recv, y_sem, local):
    g, j, p, q, w = position()
    to_g, to_j = j // 32, (4 * (j % 4) + g) * 8 + (j // 4) % 8
    from_g, from_j = p % 4, 4 * w + p // 4
    away = jnp.logical_or(to_g != g, to_j != j)

    def greet(d, carry):
        t = (w + d) % ROWS
        signal(t // 8, 8 * p + t % 8)
        return carry

    lax.fori_loop(1, ROWS, greet, 0)
    barrier = pltpu.get_barrier_semaphore()

    @pl.when(away)
    def _():
        signal(from_g, from_j)

    pl.semaphore_wait(barrier, ROWS - 1 + away.astype(jnp.int32))

    def big(d):
        t = (w + d) % ROWS
        return copy_to(lines.at[t], out.at[q, g], send.at[d], recv.at[w], t // 8, 8 * p + t % 8)

    def landed(d):
        s = (w + ROWS - d) % ROWS
        return copy_to(lines.at[s], out.at[s % 8, s // 8], send.at[d], recv.at[s], s // 8, 8 * p + s % 8)

    def small(d):
        t = (q + d) % 8
        return copy_to(params, z_params.at[q], z_send.at[d], z_recv.at[q], g, 8 * p + t)

    def small_landed(d):
        s = (q + 8 - d) % 8
        return copy_to(params, z_params.at[s], z_send.at[d], z_recv.at[s], g, 8 * p + s)

    def loop(start, stop, act):
        def body(d, carry):
            act(d)
            return carry

        lax.fori_loop(start, stop, body, 0)

    far = copy_to(params, y_params, y_sem.at[0], y_sem.at[1], to_g, to_j)
    own_line = pltpu.make_async_copy(lines.at[w], out.at[q, g], local.at[0])
    own_z = pltpu.make_async_copy(params, z_params.at[q], local.at[1])
    own_y = pltpu.make_async_copy(params, y_params, local.at[2])

    @pl.when(away)
    def _():
        far.start()

    @pl.when(jnp.logical_not(away))
    def _():
        own_y.start()

    loop(1, 8, lambda d: small(d).start())
    loop(1, ROWS, lambda d: big(d).start())
    own_line.start()
    own_z.start()
    own_line.wait()
    own_z.wait()

    @pl.when(away)
    def _():
        far.wait_send()
        copy_to(params, y_params, y_sem.at[0], y_sem.at[1], from_g, from_j).wait_recv()

    @pl.when(jnp.logical_not(away))
    def _():
        own_y.wait()

    loop(1, 8, lambda d: small(d).wait_send())
    loop(1, 8, lambda d: small_landed(d).wait_recv())
    loop(1, ROWS, lambda d: big(d).wait_send())
    loop(1, ROWS, lambda d: landed(d).wait_recv())


def send_xy(blocks, out, send, recv, local):
    g, j, p, q, w = position()

    def greet(d, carry):
        signal(g, 8 * ((p + d) % PLACES) + q)
        return carry

    lax.fori_loop(1, PLACES, greet, 0)
    pl.semaphore_wait(pltpu.get_barrier_semaphore(), PLACES - 1)
    move_xy(blocks, out, send, recv, local)


def move_xy(blocks, out, send, recv, local):
    g, j, p, q, w = position()

    def big(d):
        t = (p + d) % PLACES
        return copy_to(blocks.at[t], out.at[p], send.at[d], recv.at[p], g, 8 * t + q)

    def landed(d):
        s = (p + PLACES - d) % PLACES
        return copy_to(blocks.at[s], out.at[s], send.at[d], recv.at[s], g, 8 * s + q)

    def loop(act):
        def body(d, carry):
            act(d)
            return carry

        lax.fori_loop(1, PLACES, body, 0)

    own = pltpu.make_async_copy(blocks.at[p], out.at[p], local.at[0])
    loop(lambda d: big(d).start())
    own.start()
    own.wait()
    loop(lambda d: big(d).wait_send())
    loop(lambda d: landed(d).wait_recv())


def send_back_xy(blocks, terms, out, projections, send, recv, local, t_send, t_recv):
    g, j, p, q, w = position()
    to_j = 4 * w + p // 4
    from_g = j // 32

    def from_j(b):
        return 8 * (4 * (j % 4) + b) + (j // 4) % 8

    def greet(d, carry):
        signal(g, 8 * ((p + d) % PLACES) + q)
        return carry

    lax.fori_loop(1, PLACES, greet, 0)
    for b in range(4):

        @pl.when(jnp.logical_or(from_g != g, from_j(b) != j))
        def _():
            signal(from_g, from_j(b))

    greeted = PLACES + 3 - (to_j == j).astype(jnp.int32)
    pl.semaphore_wait(pltpu.get_barrier_semaphore(), greeted)

    for b in range(4):
        own = pltpu.make_async_copy(terms.at[pl.ds(2 * b, 2)], projections.at[:, p % 4], local.at[1])
        copy = copy_to(
            terms.at[pl.ds(2 * b, 2)], projections.at[:, p % 4], t_send.at[b], t_recv.at[p % 4], b, to_j
        )

        @pl.when(jnp.logical_or(g != b, to_j != j))
        def _():
            copy.start()

        @pl.when(jnp.logical_not(jnp.logical_or(g != b, to_j != j)))
        def _():
            own.start()
            own.wait()

    move_xy(blocks, out, send, recv, local)
    for b in range(4):
        sent = copy_to(
            terms.at[pl.ds(2 * b, 2)], projections.at[:, p % 4], t_send.at[b], t_recv.at[p % 4], b, to_j
        )
        came = copy_to(
            terms.at[pl.ds(2 * b, 2)], projections.at[:, b], t_send.at[b], t_recv.at[b], from_g, from_j(b)
        )

        @pl.when(jnp.logical_or(g != b, to_j != j))
        def _():
            sent.wait_send()

        @pl.when(jnp.logical_or(from_g != g, from_j(b) != j))
        def _():
            came.wait_recv()


def send_back_z(lines, out, send, recv, local):
    g, j, p, q, w = position()

    def greet(d, carry):
        t = (w + d) % ROWS
        signal(t // 8, 8 * p + t % 8)
        return carry

    lax.fori_loop(1, ROWS, greet, 0)
    pl.semaphore_wait(pltpu.get_barrier_semaphore(), ROWS - 1)

    def big(d):
        t = (w + d) % ROWS
        return copy_to(lines.at[t % 8, t // 8], out.at[w], send.at[d], recv.at[w], t // 8, 8 * p + t % 8)

    def landed(d):
        s = (w + ROWS - d) % ROWS
        return copy_to(lines.at[s % 8, s // 8], out.at[s], send.at[d], recv.at[s], s // 8, 8 * p + s % 8)

    def loop(act):
        def body(d, carry):
            act(d)
            return carry

        lax.fori_loop(1, ROWS, body, 0)

    own = pltpu.make_async_copy(lines.at[q, g], out.at[w], local.at[0])
    loop(lambda d: big(d).start())
    own.start()
    own.wait()
    loop(lambda d: big(d).wait_send())
    loop(lambda d: landed(d).wait_recv())


def communicate(body, number, outs, semaphores, operands):
    return pl.pallas_call(
        body,
        out_shape=outs,
        in_specs=[pl.BlockSpec(memory_space=pl.ANY)] * len(operands),
        out_specs=jax.tree.map(lambda _: pl.BlockSpec(memory_space=pl.ANY), outs),
        scratch_shapes=[pltpu.SemaphoreType.DMA((n,)) for n in semaphores],
        compiler_params=pltpu.CompilerParams(collective_id=number, has_side_effects=True),
    )(*operands)


def local(volume, x_offsets, x_fracs, z_offsets, z_fracs, y_offsets, y_fracs, slopes):
    array = lambda *shape: jax.ShapeDtypeStruct(shape, F32)
    vmem, smem = pltpu.VMEM, pltpu.SMEM
    lines, params = compute(
        shear_x,
        (array(ROWS * PLANES, 128), array(8, 128)),
        [vmem((PLANES, 384), F32)],
        (
            x_offsets,
            x_fracs,
            y_offsets.reshape(1, 32),
            y_fracs.reshape(1, 32),
            z_offsets,
            z_fracs,
            volume.reshape(PLANES, ROWS, 128),
        ),
        (smem, smem, vmem, vmem, smem, smem, vmem),
    )
    gathered, z_params, y_params = communicate(
        send_z,
        0,
        (array(8, 4, PLANES, 128), array(8, 8, 128), array(8, 128)),
        (ROWS, ROWS, 8, 8, 2, 3),
        (lines.reshape(ROWS, PLANES, 128), params),
    )
    blocks = compute(
        shear_z,
        array(PLACES, 10, 8, 128),
        [vmem((8, 256), F32), vmem((8 * DEPTH, 128), F32)],
        (gathered.reshape(8, DEPTH, 128), z_params),
        (vmem, vmem),
    )
    columns = communicate(send_xy, 1, array(PLACES, 10, 8, 128), (PLACES, PLACES, 1), (blocks,))
    turned, terms = compute(
        shear_y,
        (array(PLACES, 10, 8, 128), array(TILTS, 8, 128)),
        [
            vmem((8, 256), F32),
            vmem((8 * DEPTH, 128), F32),
            vmem((8 * DEPTH, 128), F32),
            vmem((2 * SLOPE + 1, 8, 128), F32),
        ],
        (slopes, columns, y_params),
        (smem, vmem, vmem),
    )
    back, projections = communicate(
        send_back_xy,
        2,
        (array(PLACES, 10, 8, 128), array(2, 4, 8, 128)),
        (PLACES, PLACES, 2, 4, 4),
        (turned, terms),
    )
    rows = compute(turn_back, array(8 * DEPTH, 128), [], (back,), (vmem,))
    landed = communicate(
        send_back_z,
        3,
        array(ROWS, PLANES, 128),
        (ROWS, ROWS, 1),
        (rows.reshape(8, 4, PLANES, 128),),
    )
    rotated = compute(restore, array(PLANES, ROWS, 128), [], (landed.reshape(ROWS * PLANES, 128),), (vmem,))
    return rotated.reshape(PLANES, 1, ROWS * 128), projections.reshape(2, 32, 128)


def solution(mesh):
    return jax.shard_map(
        local,
        mesh=mesh,
        in_specs=(P("gz", "gy", None), P(), P(), P("gy"), P("gy"), P("gy"), P("gy"), P()),
        out_specs=(P("gz", "gy", None), P("gz", "gy", None)),
        check_vma=False,
    )
```

time: 382 us -> 153 us (0.40); the launches traced: 374 us -> 151 us
  local copies, waits for them, and re-layouts: 171 us -> 12 us
  Pallas kernels: 0 us -> 137 us
  waiting for transfers between devices: 96 us -> 0 us
  matrix products: 44.2 us -> 0 us
  starting transfers between devices: 30.3 us -> 0 us
  other arithmetic: 16.3 us -> 0 us
  between operations: 16 us -> 2.11 us
    gather x128 -> x0, local copies, waits for them, and re-layouts: 147 us -> none
    pallas_call x0 -> x9, Pallas kernels: none -> 137 us  [the longest x4 121 us: communicate(): pl.pallas_call(body, out_shape=outs, in_specs=[pl.BlockSpec(memory_space=...]
    ppermute x2 -> x0, waiting for transfers between devices: 49.5 us -> none  [the longest x1 43 us: with_halo(): after = lax.ppermute(first, axis, down)]
    dot_general x3 -> x0, matrix products: 44.2 us -> none  [the longest x1 27.8 us: shear_lines(): jnp.einsum('prbj,pji->prbi', windows, band_matrix, precision=lax.Precisio...]
    reduce_scatter x1 -> x0, waiting for transfers between devices: 28.2 us -> none  [local(): lax.psum_scatter(partial_terms, 'gz', scatter_dimension=0, tiled=True)]
    all_to_all x2 -> x0, starting transfers between devices: 19.4 us -> none  [the longest x1 9.74 us: local(): lax.all_to_all(outgoing, 'gy', split_axis=0, concat_axis=1, tiled=True)]
    all_to_all x2 -> x0, waiting for transfers between devices: 18.2 us -> none  [the longest x1 18.2 us: local(): lax.all_to_all(outgoing, 'gy', split_axis=0, concat_axis=1, tiled=True)]
    ppermute x2 -> x0, starting transfers between devices: 10.9 us -> none  [the longest x1 9.63 us: with_halo(): before = lax.ppermute(last, axis, up)]
  transfers between devices with their start and end apart: 5 -> 0, of which waited for: 4 -> 0; matrix products, arithmetic and copies ran while one was open for 23% -> 0% of each run, Pallas kernels for 0% -> 0%
where the time goes in v1:
time: 153 us; the launch traced here: 151 us
  Pallas kernels  137 us (90%)
  local copies, waits for them, and re-layouts  12 us (8%)
  between operations  2.11 us (1%)
    pallas_call x4, Pallas kernels, communicate(): pl.pallas_call(body, out_shape=outs, in_specs=[pl.BlockSpec(memory_space=...  121 us
    pallas_call x5, Pallas kernels, compute(): pl.pallas_call(body, out_shape=outs, in_specs=[pl.BlockSpec(memory_space=...  15.5 us
    unnamed x39, local copies, waits for them, and re-layouts  12 us

profile of v1, /device:TPU:25, one launch (start us, length us, event | category | flops | bytes accessed | tf_op | source)
XLA Modules:
  0.0 150.8 jit_solution(6537986396406307678)
XLA Ops:
  2.0 0.6 copy-done.14
  2.6 0.0 copy-done.13
  2.6 1.1 copy-done.4
  3.7 5.3 %shard_map.95 = (f32[1280,128]{1,0:T(8,128)S(1)}, f32[8,128]{1,0:T(8,128)S(1)}) custom-call(s32[160]{0:T(256)S(1)} %copy-done.13, f32[160]{0:T(256)S(1)} %copy-done.14, s32[1,32]{1,0:T(1,128)S(1)} %bitcast.14, f32[1,32]{1,0:T(1,128)S(1)} %bitcast.15, s32[1]{0:T(128)S(6)} %copy.12.z_off, f32[1]{0:T(128)S(6)} %copy.13.z_frac, f32[40,32,128]{2,1,0:T(8,128)S(1)} %bitcast.11), custom_call_target="tpu_custom_call" | custom-call | tf_op jit(solution)/shard_map/pallas_call | solution.py:182
  9.0 0.8 copy-done.5
  9.9 0.6 copy-done.12
  10.4 51.4 %shard_map.96 = (f32[8,4,40,128]{3,2,1,0:T(8,128)}, f32[8,8,128]{2,1,0:T(8,128)}, f32[8,128]{1,0:T(8,128)}) custom-call(f32[32,40,128]{2,1,0:T(8,128)} %bitcast.12, f32[8,128]{1,0:T(8,128)} %copy-done.12), custom_call_target="tpu_custom_call" | custom-call | tf_op jit(solution)/shard_map/pallas_call | solution.py:422
  61.9 1.1 copy-done.7
  62.9 0.8 copy-done.10
  63.7 1.1 shard_map.97.blocks
  64.8 0.8 copy-done.1
  65.7 12.5 %shard_map.98.blocks = f32[16,10,8,128]{3,2,1,0:T(8,128)} custom-call(f32[16,10,8,128]{3,2,1,0:T(8,128)} %copy-done.1), custom_call_target="tpu_custom_call" | custom-call | tf_op jit(solution)/shard_map/pallas_call | solution.py:422
  78.2 1.1 copy-done
  79.3 7.7 %shard_map.99 = (f32[16,10,8,128]{3,2,1,0:T(8,128)S(1)}, f32[8,8,128]{2,1,0:T(8,128)S(1)}) custom-call(s32[8]{0:T(128)S(1)} %copy-done.17, f32[16,10,8,128]{3,2,1,0:T(8,128)S(1)} %copy-done, f32[8,128]{1,0:T(8,128)S(1)} %copy-done.11), custom_call_target="tpu_custom_call" | custom-call | tf_op jit(solution)/shard_map/pallas_call | solution.py:182
  87.0 0.8 copy-done.6
  87.9 0.6 copy-done.9
  88.5 16.8 %shard_map.100 = (f32[16,10,8,128]{3,2,1,0:T(8,128)}, f32[2,4,8,128]{3,2,1,0:T(8,128)}) custom-call(f32[16,10,8,128]{3,2,1,0:T(8,128)} %copy-done.6, f32[8,8,128]{2,1,0:T(8,128)} %copy-done.9), custom_call_target="tpu_custom_call" | custom-call | tf_op jit(solution)/shard_map/pallas_call | solution.py:422
  105.3 1.1 copy-done.8
  106.4 0.4 shard_map.101
  106.8 0.8 copy-done.2
  107.6 40.5 %shard_map.102 = f32[32,40,128]{2,1,0:T(8,128)} custom-call(f32[8,4,40,128]{3,2,1,0:T(8,128)} %bitcast.9), custom_call_target="tpu_custom_call" | custom-call | tf_op jit(solution)/shard_map/pallas_call | solution.py:422
  148.1 1.1 copy-done.3
  149.2 1.0 shard_map.103
  150.2 0.6 copy.14
  (24 shorter events, 0.1 us)
Async XLA Ops:
  1.9 0.7 copy-start.14
  1.9 0.7 copy-start.16
  1.9 0.7 copy-start.13
  2.0 0.7 copy-start.15
  2.6 1.1 copy-start.4
  9.0 0.8 copy-start.5
  9.9 0.6 copy-start.12
  61.8 1.1 copy-start.7
  62.9 0.8 copy-start.10
  64.8 0.8 copy-start.1
  65.6 12.5 %copy-start.11 = (f32[8,128]{1,0:T(8,128)S(1)}, f32[8,128]{1,0:T(8,128)}, u32[]{:S(2)}) copy-start(f32[8,128]{1,0:T(8,128)} %get-tuple-element.15.params) | copy-start | bytes 12292
  65.7 12.5 %copy-start.17 = (s32[8]{0:T(128)S(1)}, s32[8]{0:T(128)}, u32[]{:S(2)}) copy-start(s32[8]{0:T(128)} %slopes.1) | copy-start | bytes 100
  78.2 1.1 copy-start
  87.0 0.8 copy-start.6
  87.9 0.6 copy-start.9
  105.3 1.1 copy-start.8
  106.8 0.8 copy-start.2
  148.1 1.1 copy-start.3
  149.2 1.0 copy-start.18

commit v2 on v0

v2 whole, which is shorter than its diff:
```python
import functools

import jax
import jax.numpy as jnp
from jax import lax
from jax.experimental import pallas as pl
from jax.experimental.pallas import tpu as pltpu
from jax.sharding import PartitionSpec as P

TAPS = 64
ROWS = 32
PLANES = 40
DEPTH = 160
PLACES = 16
TILTS = 8
SLOPE = 4
F32 = jnp.float32
BF16 = jnp.bfloat16
VMEM_BYTES = 48 * 1024 * 1024


def tap_weight(offset, fraction):
    moved = offset.astype(F32) - fraction
    inside = (offset >= 1 - TAPS // 2) & (offset <= TAPS // 2)
    angle = jnp.pi * moved
    centre = moved == 0.0
    ratio = jnp.sin(angle) / jnp.where(centre, 1.0, angle)
    sinc = jnp.where(centre, 1.0, ratio)
    value = sinc * (0.5 + 0.5 * jnp.cos(jnp.pi * moved / (TAPS // 2 + 1)))
    return jnp.where(inside, value, 0.0)


def halves(value):
    high = value.astype(BF16)
    return high, (value - high.astype(F32)).astype(BF16)


def product(left, right):
    left_high, left_low = left
    right_high, right_low = right
    dot = functools.partial(jnp.dot, preferred_element_type=F32)
    return dot(left_high, right_high) + (dot(left_low, right_high) + dot(left_high, right_low))


def iota(shape, axis):
    return lax.broadcasted_iota(jnp.int32, shape, axis)


def band(row, rows, start=0, step=1):
    wide = jnp.broadcast_to(row, (rows, row.shape[1]))
    return pltpu.roll(wide, start, 1, stride=step, stride_axis=0)


def block(ref, index):
    return ref.at[pl.ds(pl.multiple_of(PLANES * index, 8), PLANES)]


def loop(start, stop, act):
    def body(d, carry):
        act(d)
        return carry

    lax.fori_loop(start, stop, body, 0)


def shear_x(offs, fracs, planes, arrive, out, taps):
    first = lax.axis_index("gz") * PLANES
    sub = iota((8, 128), 0)
    for part in range(PLANES // 8):
        off = jnp.zeros((8, 128), jnp.int32)
        frac = jnp.zeros((8, 128), F32)
        for s in range(8):
            off = jnp.where(sub == s, offs[first + 8 * part + s], off)
            frac = jnp.where(sub == s, fracs[first + 8 * part + s], frac)
        for side in range(2):
            lane = iota((8, 128), 1) + 128 * side
            weights = tap_weight(128 - lane - off, frac)
            taps[8 * part : 8 * part + 8, 128 * side : 128 * side + 128] = weights
        taps[8 * part : 8 * part + 8, 256:384] = jnp.zeros((8, 128), F32)
    row = iota((ROWS, 128), 0)

    def plane(z, carry):
        matrix = band(taps[pl.ds(z, 1), :], 128)
        total = product(halves(planes[z]), halves(matrix))
        after = jnp.where(row < ROWS - 1, pltpu.roll(total[:, :128], ROWS - 1, 0), 0.0)
        before = jnp.where(row > 0, pltpu.roll(total[:, 256:], 1, 0), 0.0)
        out[pl.ds(z, ROWS, stride=PLANES), :] = total[:, 128:256] + (after + before)
        return carry

    arrive()
    lax.fori_loop(0, PLANES, plane, 0, unroll=4)


def shear_z(h, lines, params, out, taps, mixed):
    lane = iota((8, 256), 1)
    target = jnp.where(lane < DEPTH, lane, lane - 256)
    off = params[:, 2, :][:, 0:1].astype(jnp.int32)
    frac = params[:, 3, :][:, 0:1]
    taps[0:4, :] = tap_weight(target[0:4] - off, frac)
    for n in range(4):
        source = halves(lines[640 * h + DEPTH * n : 640 * h + DEPTH * n + DEPTH, :])
        for odd in range(2):
            matrix = band(taps[n : n + 1, :], DEPTH // 2, odd, 2)[:, :DEPTH]
            value = product(halves(matrix), source)
            mixed[pl.ds(2 * n + odd, DEPTH // 2, stride=8), :] = value
    for part in range(5):
        turned = mixed[128 * part : 128 * part + 128, :].T
        for p in range(PLACES):
            row = 640 * h + PLANES * p + 8 * part
            out[row : row + 8, :] = turned[8 * p : 8 * p + 8, :]


def exchange(values):
    lane = iota((8, 128), 1)
    values = list(values)
    for step in (1, 2, 4, 8, 16):
        shift = 1 if step == 1 else 4 * step
        keep = (lane // shift) % 2 == 0
        for low in range(32):
            if low & step == 0:
                a, b = values[low], values[low | step]
                values[low] = jnp.where(keep, a, pltpu.roll(b, shift, 1))
                values[low | step] = jnp.where(keep, pltpu.roll(a, 128 - shift, 1), b)
    return values


def tile(ref, index):
    return ref.at[pl.ds(pl.multiple_of(8 * index, 8), 8)]


def shear_y(blocks, params, out, taps, before, after):
    def unpack(part):
        values = exchange([tile(blocks, 5 * i + part)[...] for i in range(32)])
        for i in range(32):
            tile(before, 32 * part + i)[...] = values[i]

    loop(0, 5, unpack)
    start = 8 * (lax.axis_index("gy") // 8 % 4)
    pick = iota((8, 128), 1) == start + iota((8, 128), 0)
    off = jnp.sum(jnp.where(pick, params[0:1, :], 0.0), axis=1, keepdims=True)
    frac = jnp.sum(jnp.where(pick, params[1:2, :], 0.0), axis=1, keepdims=True)
    lane = iota((8, 256), 1)
    target = jnp.where(lane < 128, lane, lane - 256)
    taps[...] = tap_weight(-target - off.astype(jnp.int32), frac)

    for x in range(8):
        matrix = band(taps[x : x + 1, :], 128)[:, :128]
        value = product(halves(before[pl.ds(x, DEPTH, stride=8), :]), halves(matrix))
        after[pl.ds(x, DEPTH, stride=8), :] = value

    def pack(part):
        values = exchange([tile(after, 32 * part + i)[...] for i in range(32)])
        for i in range(32):
            tile(out, 5 * i + part)[...] = values[i]

    loop(0, 5, pack)


def project(slopes, after, projections, table):
    lane = iota((8, 128), 1)
    zero = jnp.zeros((8, 128), F32)
    count = 2 * SLOPE + 1
    sums, totals = [zero] * count, [zero] * count
    for z in range(DEPTH):
        value = after[8 * z : 8 * z + 8, :]
        for i in range(count):
            lift = (i - SLOPE) * (2 * z - DEPTH) * 128 // (16 * DEPTH)
            following = (i - SLOPE) * (2 * z + 2 - DEPTH) * 128 // (16 * DEPTH)
            sums[i] = sums[i] + value
            if z == DEPTH - 1 or lift != following:
                moved = sums[i]
                if lift > 0:
                    moved = jnp.where(lane < 128 - lift, pltpu.roll(moved, 128 - lift, 1), 0.0)
                elif lift < 0:
                    moved = jnp.where(lane >= -lift, pltpu.roll(moved, -lift, 1), 0.0)
                totals[i] = totals[i] + moved
                sums[i] = zero
    for i in range(count):
        table[i] = totals[i] * DEPTH ** (-0.5)
    for t in range(TILTS):
        projections[t] = table[slopes[t] + SLOPE]


def turn_back(h, blocks, out, turned):
    for part in range(5):
        tiles = [blocks[640 * h + 40 * p + 8 * part : 640 * h + 40 * p + 8 * part + 8, :] for p in range(PLACES)]
        turned[128 * part : 128 * part + 128, :] = jnp.concatenate(tiles, axis=0).T
    for n in range(4):
        for odd in range(2):
            value = turned[pl.ds(2 * n + odd, DEPTH // 2, stride=8), :]
            out[pl.ds(640 * h + DEPTH * n + odd, DEPTH // 2, stride=2), :] = value


def restore(lines, out):
    for z in range(PLANES):
        out[z] = lines[pl.ds(z, ROWS, stride=PLANES), :]


def copy_to(src, dst, send, recv, g, j):
    return pltpu.make_async_remote_copy(
        src_ref=src,
        dst_ref=dst,
        send_sem=send,
        recv_sem=recv,
        device_id={"gz": g, "gy": j},
        device_id_type=pl.DeviceIdType.MESH,
    )


def signal(g, j):
    pl.semaphore_signal(
        pltpu.get_barrier_semaphore(),
        inc=1,
        device_id={"gz": g, "gy": j},
        device_id_type=pl.DeviceIdType.MESH,
    )


def rotate(
    x_offs, x_fracs, z_off, z_frac, slopes, y_offs, y_fracs, volume,
    landed, projections,
    planes, lines, gathered, mixed, outgoing, columns, before, after, returning, returned, rows,
    params, z_params, y_params, x_taps, z_taps, y_taps, table, terms,
    load, local, z_send, z_recv, xy_send, xy_recv, back_send, back_recv, home_send, home_recv,
    p_send, p_recv, t_send, t_recv,
):
    g, j = lax.axis_index("gz"), lax.axis_index("gy")
    p, n, core = j // 8, (j // 2) % 4, j % 2
    w = 4 * g + n

    def at_z(t):
        return t // 4, 8 * p + 2 * (t % 4) + core

    def at_xy(t, c):
        return g, 8 * t + 2 * n + c

    row = 16 * core + w
    home_j = 4 * row + p // 4
    owner_g = (j // 4) % 16 // 4

    def owner_j(b):
        return 8 * (4 * (j % 4) + b) + 2 * ((j // 4) % 4) + j // 64

    def is_self(a, b):
        return jnp.logical_and(a == g, b == j)

    loads = [
        pltpu.make_async_copy(volume.at[pl.ds(8 * i, 8)], planes.at[pl.ds(8 * i, 8)], load.at[i]) for i in range(5)
    ]
    for item in loads:
        item.start()
    loop(1, PLACES, lambda d: signal(*at_z((w + d) % PLACES)))
    for c in range(2):
        loop(1, PLACES, lambda d: signal(*at_xy((p + d) % PLACES, c)))
    signal(*at_xy(p, 1 - core))
    mine = is_self(owner_g, owner_j(g))
    for b in range(4):
        pl.when(jnp.logical_not(is_self(owner_g, owner_j(b))))(lambda b=b: signal(owner_g, owner_j(b)))
    own_home = is_self(p % 4, home_j)
    pl.when(jnp.logical_not(own_home))(lambda: signal(p % 4, home_j))

    params[...] = jnp.zeros((8, 128), F32)
    params[0:1, 0:32] = y_offs[...].astype(F32)
    params[1:2, 0:32] = y_fracs[...]
    params[2:3, :] = jnp.full((1, 128), z_off[0], jnp.int32).astype(F32)
    params[3:4, :] = jnp.full((1, 128), z_frac[0], F32)

    def arrive():
        for item in loads:
            item.wait()

    shear_x(x_offs, x_fracs, planes, arrive, lines, x_taps)
    greeted = 15 + 31 + 5 - (home_j == j).astype(jnp.int32) - mine.astype(jnp.int32)
    pl.semaphore_wait(pltpu.get_barrier_semaphore(), greeted)

    def z_param(d):
        t = 4 * g + (n + d) % 4
        return copy_to(params, z_params.at[n], p_send.at[d], p_recv.at[n], *at_z(t))

    def z_param_in(d):
        s = (n + 4 - d) % 4
        return copy_to(params, z_params.at[s], p_send.at[d], p_recv.at[s], *at_z(4 * g + s))

    y_out = copy_to(params, y_params, p_send.at[4], p_recv.at[4], owner_g, owner_j(g))
    y_in = copy_to(params, y_params, p_send.at[4], p_recv.at[4], p % 4, home_j)
    y_own = pltpu.make_async_copy(params, y_params, local.at[0])
    z_own = pltpu.make_async_copy(params, z_params.at[n], local.at[1])
    loop(1, 4, lambda d: z_param(d).start())
    pl.when(jnp.logical_not(mine))(lambda: y_out.start())
    pl.when(mine)(lambda: y_own.start())
    z_own.start()

    def z_out(h, d):
        t = (w + d) % PLACES
        dst = block(gathered, 16 * h + 4 * n + g)
        return copy_to(block(lines, 16 * h + t), dst, z_send.at[h, d], z_recv.at[h, w], *at_z(t))

    def z_in(h, d):
        s = (w + PLACES - d) % PLACES
        dst = block(gathered, 16 * h + 4 * (s % 4) + s // 4)
        return copy_to(block(lines, 16 * h + s), dst, z_send.at[h, d], z_recv.at[h, s], *at_z(s))

    z_owns = [
        pltpu.make_async_copy(block(lines, 16 * h + w), block(gathered, 16 * h + 4 * n + g), local.at[2 + h])
        for h in range(2)
    ]
    for h in range(2):
        loop(1, PLACES, lambda d: z_out(h, d).start())
        z_owns[h].start()
    z_own.wait()
    loop(1, 4, lambda d: z_param_in(d).wait_recv())

    def xy_out(h, d):
        t = (p + d) % PLACES
        dst = block(columns, 2 * p + core)
        return copy_to(block(outgoing, 16 * h + t), dst, xy_send.at[h, d], xy_recv.at[2 * p + core], *at_xy(t, h))

    def xy_in(c, d):
        s = (p + PLACES - d) % PLACES
        src = block(outgoing, 16 * core + s)
        return copy_to(src, block(columns, 2 * s + c), xy_send.at[0, d], xy_recv.at[2 * s + c], *at_xy(s, c))

    xy_own = pltpu.make_async_copy(block(outgoing, 16 * core + p), block(columns, 2 * p + core), local.at[4])

    def middle(h):
        z_owns[h].wait()
        loop(1, PLACES, lambda d: z_in(h, d).wait_recv())
        shear_z(h, gathered, z_params, outgoing, z_taps, mixed)
        loop(1, PLACES, lambda d: xy_out(h, d).start())
        pl.when(core != h)(lambda: xy_out(h, 0).start())
        pl.when(core == h)(lambda: xy_own.start())

    def back_out(c, d):
        t = (p + d) % PLACES
        dst = block(returned, 16 * core + p)
        return copy_to(block(returning, 2 * t + c), dst, back_send.at[c, d], back_recv.at[core, p], *at_xy(t, c))

    def back_in(h, d):
        s = (p + PLACES - d) % PLACES
        src = block(returning, 2 * s + core)
        return copy_to(src, block(returned, 16 * h + s), back_send.at[0, d], back_recv.at[h, s], *at_xy(s, h))

    back_own = pltpu.make_async_copy(block(returning, 2 * p + core), block(returned, 16 * core + p), local.at[5])

    def columns_here():
        for c in range(2):
            loop(1, PLACES, lambda d: xy_in(c, d).wait_recv())
        xy_in(1 - core, 0).wait_recv()
        xy_own.wait()
        shear_y(columns, y_params, returning, y_taps, before, after)
        for c in range(2):
            loop(1, PLACES, lambda d: back_out(c, d).start())
        back_out(1 - core, 0).start()
        back_own.start()

    def home_out(h, d):
        t = (w + d) % PLACES
        src = block(rows, 16 * h + 4 * (t % 4) + t // 4)
        return copy_to(src, block(landed, 16 * h + w), home_send.at[h, d], home_recv.at[h, w], *at_z(t))

    def home_in(h, d):
        s = (w + PLACES - d) % PLACES
        src = block(rows, 16 * h + 4 * (s % 4) + s // 4)
        return copy_to(src, block(landed, 16 * h + s), home_send.at[h, d], home_recv.at[h, s], *at_z(s))

    home_owns = [
        pltpu.make_async_copy(block(rows, 16 * h + 4 * n + g), block(landed, 16 * h + w), local.at[6 + h])
        for h in range(2)
    ]

    def finish(h):
        loop(1, PLACES, lambda d: back_in(h, d).wait_recv())
        pl.when(core != h)(lambda: back_in(h, 0).wait_recv())
        pl.when(core == h)(lambda: back_own.wait())
        turn_back(h, returned, rows, mixed)
        loop(1, PLACES, lambda d: home_out(h, d).start())
        home_owns[h].start()

    middle(0)
    pl.when(jnp.logical_not(own_home))(lambda: y_in.wait_recv())
    pl.when(mine)(lambda: y_own.wait())
    pl.when(core == 0)(columns_here)
    middle(1)
    finish(0)
    pl.when(core == 1)(columns_here)
    finish(1)

    project(slopes, after, terms, table)

    def term_out(b):
        return copy_to(
            terms.at[pl.ds(2 * b, 2)], projections.at[:, p % 4], t_send.at[b], t_recv.at[p % 4], b, home_j
        )

    def term_in(b):
        return copy_to(
            terms.at[pl.ds(2 * b, 2)], projections.at[:, b], t_send.at[b], t_recv.at[b], owner_g, owner_j(b)
        )

    def term_own():
        return pltpu.make_async_copy(terms.at[pl.ds(2 * g, 2)], projections.at[:, p % 4], local.at[0])

    for b in range(4):
        pl.when(jnp.logical_not(is_self(b, home_j)))(lambda b=b: term_out(b).start())
    pl.when(home_j == j)(lambda: term_own().start())

    loop(1, 4, lambda d: z_param(d).wait_send())
    pl.when(jnp.logical_not(mine))(lambda: y_out.wait_send())
    for h in range(2):
        loop(1, PLACES, lambda d: z_out(h, d).wait_send())
        loop(1, PLACES, lambda d: xy_out(h, d).wait_send())
        pl.when(core != h)(lambda h=h: xy_out(h, 0).wait_send())
        loop(1, PLACES, lambda d: back_out(h, d).wait_send())
    back_out(1 - core, 0).wait_send()
    pl.when(home_j == j)(lambda: term_own().wait())
    for b in range(4):
        pl.when(jnp.logical_not(is_self(b, home_j)))(lambda b=b: term_out(b).wait_send())
        pl.when(jnp.logical_not(is_self(owner_g, owner_j(b))))(lambda b=b: term_in(b).wait_recv())
    for h in range(2):
        loop(1, PLACES, lambda d: home_out(h, d).wait_send())
        home_owns[h].wait()
        loop(1, PLACES, lambda d: home_in(h, d).wait_recv())


def local(volume, x_offsets, x_fracs, z_offsets, z_fracs, y_offsets, y_fracs, slopes):
    array = lambda *shape: jax.ShapeDtypeStruct(shape, F32)
    vmem = lambda *shape: pltpu.VMEM(shape, F32)
    many = lambda *shape: pltpu.SemaphoreType.DMA(shape)
    smem = pltpu.SMEM
    whole = ROWS * PLANES
    spaces = (smem, smem, smem, smem, smem, pltpu.VMEM, pltpu.VMEM, pl.ANY)
    landed, projections = pl.pallas_call(
        rotate,
        out_shape=(array(whole, 128), array(2, 4, 8, 128)),
        in_specs=[pl.BlockSpec(memory_space=space) for space in spaces],
        out_specs=[pl.BlockSpec(memory_space=pl.ANY)] * 2,
        scratch_shapes=[
            vmem(PLANES, ROWS, 128),
            vmem(whole, 128),
            vmem(whole, 128),
            vmem(whole // 2, 128),
            *[vmem(whole, 128)] * 7,
            vmem(8, 128),
            vmem(4, 8, 128),
            vmem(8, 128),
            vmem(PLANES, 384),
            vmem(8, 256),
            vmem(8, 256),
            vmem(2 * SLOPE + 1, 8, 128),
            vmem(TILTS, 8, 128),
            many(5),
            many(8),
            many(2, PLACES),
            many(2, PLACES),
            many(2, PLACES),
            many(2 * PLACES),
            many(2, PLACES),
            many(2, PLACES),
            many(2, PLACES),
            many(2, PLACES),
            many(5),
            many(5),
            many(4),
            many(4),
        ],
        compiler_params=pltpu.CompilerParams(
            vmem_limit_bytes=VMEM_BYTES, collective_id=0, has_side_effects=True
        ),
    )(
        x_offsets,
        x_fracs,
        z_offsets,
        z_fracs,
        slopes,
        y_offsets.reshape(1, 32),
        y_fracs.reshape(1, 32),
        volume.reshape(PLANES, ROWS, 128),
    )
    rotated = pl.pallas_call(
        restore,
        out_shape=array(PLANES, ROWS, 128),
        in_specs=[pl.BlockSpec(memory_space=pltpu.VMEM)],
        compiler_params=pltpu.CompilerParams(vmem_limit_bytes=VMEM_BYTES),
    )(landed)
    return rotated.reshape(PLANES, 1, ROWS * 128), projections.reshape(2, 32, 128)


def solution(mesh):
    return jax.shard_map(
        local,
        mesh=mesh,
        in_specs=(P("gz", "gy", None), P(), P(), P("gy"), P("gy"), P("gy"), P("gy"), P()),
        out_specs=(P("gz", "gy", None), P("gz", "gy", None)),
        check_vma=False,
    )
```

time: 382 us -> 103 us (0.27)
  the two profiles are of different devices: /device:TPU:25 before, /device:TPU:41 now
where the time goes in v2:
time: 103 us
  Pallas kernels  98.8 us (96%)
  local copies, waits for them, and re-layouts  2.39 us (2%)
  between operations  1.97 us (2%)
    pallas_call x1, Pallas kernels, local(): pl.pallas_call(rotate, out_shape=(array(whole, 128), array(2, 4, 8, 128))...  97.9 us
    unnamed x13, local copies, waits for them, and re-layouts  2.39 us

profile of v2, /device:TPU:41, one launch (start us, length us, event | category | flops | bytes accessed | tf_op | source)
XLA Modules:
  0.0 103.2 jit_solution(5549554104139692982)
XLA Ops:
  1.9 0.0 copy-start.2
  1.9 0.0 copy-start.4
  1.9 0.0 copy-start.5
  2.0 0.0 copy-start.1
  2.0 0.0 copy-start.3
  2.0 0.6 copy-done.2
  2.6 0.0 copy-done.4
  2.6 0.0 copy-done.5
  2.6 0.0 copy-done.1
  2.7 0.0 copy-done.3
  2.7 0.0 copy-start
  2.7 1.1 %copy-done = f32[40,1,4096]{2,1,0:T(1,128)S(1)} copy-done((f32[40,1,4096]{2,1,0:T(1,128)S(1)}, f32[40,1,4096]{2,1,0:T(1,128)}, u32[]{:S(2)}) %copy-start) | copy-done | bytes 655384
  3.7 97.9 %shard_map.95 = (f32[1280,128]{1,0:T(8,128)S(1)}, f32[2,4,8,128]{3,2,1,0:T(8,128)S(1)}) custom-call(s32[160]{0:T(256)S(1)} %copy-done.1, f32[160]{0:T(256)S(1)} %copy-done.2, s32[1]{0:T(128)S(6)} %copy.12.z_off, f32[1]{0:T(128)S(6)} %copy.13.z_frac, s32[8]{0:T(128)S(1)} %copy-done.3, s32[1,32]{1,0:T(1,128)S(1)} %bitcast.7, f32[1,32]{1,0:T(1,128)S(1)} %bitcast.8, ...), custom_call_target="tpu_custom_call" | custom-call | tf_op jit(solution)/shard_map/pallas_call | solution.py:432
  101.6 1.0 shard_map.96
  102.6 0.6 copy.14
Async XLA Ops:
  1.9 0.7 copy-start.2
  1.9 0.7 copy-start.4
  1.9 0.7 copy-start.5
  2.0 0.7 copy-start.1
  2.0 0.7 copy-start.3
  2.7 1.1 %copy-start = (f32[40,1,4096]{2,1,0:T(1,128)S(1)}, f32[40,1,4096]{2,1,0:T(1,128)}, u32[]{:S(2)}) copy-start(f32[40,1,4096]{2,1,0:T(1,128)} %param.8) | copy-start | bytes 1966084

commit v3 on v2

--- a/solution.py
+++ b/solution.py
@@ -12,11 +12,13 @@
 PLANES = 40
 DEPTH = 160
 PLACES = 16
+PARTS = ((0, 3), (3, 5))
 TILTS = 8
 SLOPE = 4
 F32 = jnp.float32
 BF16 = jnp.bfloat16
 VMEM_BYTES = 48 * 1024 * 1024
+ALL_VMEM_BYTES = 67043328
 
 
 def tap_weight(offset, fraction):
@@ -53,6 +55,11 @@
 
 def block(ref, index):
     return ref.at[pl.ds(pl.multiple_of(PLANES * index, 8), PLANES)]
+
+
+def part_of(ref, index, k):
+    first, last = PARTS[k]
+    return ref.at[pl.ds(pl.multiple_of(PLANES * index + 8 * first, 8), 8 * (last - first))]
 
 
 def loop(start, stop, act):
@@ -91,17 +98,23 @@
     lax.fori_loop(0, PLANES, plane, 0, unroll=4)
 
 
-def shear_z(h, lines, params, out, taps, mixed):
+def prepare_z(params, highs, lows, taps):
     lane = iota((8, 256), 1)
     target = jnp.where(lane < DEPTH, lane, lane - 256)
     off = params[:, 2, :][:, 0:1].astype(jnp.int32)
     frac = params[:, 3, :][:, 0:1]
     taps[0:4, :] = tap_weight(target[0:4] - off, frac)
     for n in range(4):
+        for odd in range(2):
+            matrix = band(taps[n : n + 1, :], DEPTH // 2, odd, 2)[:, :DEPTH]
+            highs[2 * n + odd], lows[2 * n + odd] = halves(matrix)
+
+
+def shear_z(h, lines, highs, lows, out, mixed):
+    for n in range(4):
         source = halves(lines[640 * h + DEPTH * n : 640 * h + DEPTH * n + DEPTH, :])
         for odd in range(2):
-            matrix = band(taps[n : n + 1, :], DEPTH // 2, odd, 2)[:, :DEPTH]
-            value = product(halves(matrix), source)
+            value = product((highs[2 * n + odd], lows[2 * n + odd]), source)
             mixed[pl.ds(2 * n + odd, DEPTH // 2, stride=8), :] = value
     for part in range(5):
         turned = mixed[128 * part : 128 * part + 128, :].T
@@ -128,13 +141,7 @@
     return ref.at[pl.ds(pl.multiple_of(8 * index, 8), 8)]
 
 
-def shear_y(blocks, params, out, taps, before, after):
-    def unpack(part):
-        values = exchange([tile(blocks, 5 * i + part)[...] for i in range(32)])
-        for i in range(32):
-            tile(before, 32 * part + i)[...] = values[i]
-
-    loop(0, 5, unpack)
+def prepare_y(params, highs, lows, taps):
     start = 8 * (lax.axis_index("gy") // 8 % 4)
     pick = iota((8, 128), 1) == start + iota((8, 128), 0)
     off = jnp.sum(jnp.where(pick, params[0:1, :], 0.0), axis=1, keepdims=True)
@@ -142,18 +149,29 @@
     lane = iota((8, 256), 1)
     target = jnp.where(lane < 128, lane, lane - 256)
     taps[...] = tap_weight(-target - off.astype(jnp.int32), frac)
-
     for x in range(8):
-        matrix = band(taps[x : x + 1, :], 128)[:, :128]
-        value = product(halves(before[pl.ds(x, DEPTH, stride=8), :]), halves(matrix))
-        after[pl.ds(x, DEPTH, stride=8), :] = value
+        highs[x], lows[x] = halves(band(taps[x : x + 1, :], 128)[:, :128])
+
+
+def shear_y(k, blocks, highs, lows, out, before, after):
+    first, last = PARTS[k]
+
+    def unpack(part):
+        values = exchange([tile(blocks, 5 * i + part)[...] for i in range(32)])
+        for i in range(32):
+            tile(before, 32 * part + i)[...] = values[i]
+
+    loop(first, last, unpack)
+    for x in range(8):
+        rows = pl.ds(256 * first + x, 32 * (last - first), stride=8)
+        after[rows, :] = product(halves(before[rows, :]), (highs[x], lows[x]))
 
     def pack(part):
         values = exchange([tile(after, 32 * part + i)[...] for i in range(32)])
         for i in range(32):
             tile(out, 5 * i + part)[...] = values[i]
 
-    loop(0, 5, pack)
+    loop(first, last, pack)
 
 
 def project(slopes, after, projections, table):
@@ -181,19 +199,23 @@
         projections[t] = table[slopes[t] + SLOPE]
 
 
-def turn_back(h, blocks, out, turned):
-    for part in range(5):
+def turn_back(h, k, blocks, out, turned):
+    first, last = PARTS[k]
+    for part in range(first, last):
         tiles = [blocks[640 * h + 40 * p + 8 * part : 640 * h + 40 * p + 8 * part + 8, :] for p in range(PLACES)]
         turned[128 * part : 128 * part + 128, :] = jnp.concatenate(tiles, axis=0).T
+    count = 16 * (last - first)
     for n in range(4):
         for odd in range(2):
-            value = turned[pl.ds(2 * n + odd, DEPTH // 2, stride=8), :]
-            out[pl.ds(640 * h + DEPTH * n + odd, DEPTH // 2, stride=2), :] = value
-
-
-def restore(lines, out):
-    for z in range(PLANES):
-        out[z] = lines[pl.ds(z, ROWS, stride=PLANES), :]
+            value = turned[pl.ds(128 * first + 2 * n + odd, count, stride=8), :]
+            out[pl.ds(640 * h + DEPTH * n + 32 * first + odd, count, stride=2), :] = value
+
+
+def restore(lines, terms, out, projections):
+    for z in range(8):
+        for part in range(ROWS // 8):
+            out[z, 8 * part : 8 * part + 8, :] = lines[8 * part : 8 * part + 8, z, :]
+    projections[...] = terms[...]
 
 
 def copy_to(src, dst, send, recv, g, j):
@@ -217,11 +239,13 @@
 
 
 def rotate(
-    x_offs, x_fracs, z_off, z_frac, slopes, y_offs, y_fracs, volume,
+    x_offs_in, x_fracs_in, z_off_in, z_frac_in, slopes_in, y_offs_in, y_fracs_in, volume,
     landed, projections,
     planes, lines, gathered, mixed, outgoing, columns, before, after, returning, returned, rows,
+    x_offs, x_fracs, z_off, z_frac, slopes, y_offs, y_fracs,
+    z_highs, z_lows, y_highs, y_lows,
     params, z_params, y_params, x_taps, z_taps, y_taps, table, terms,
-    load, local, z_send, z_recv, xy_send, xy_recv, back_send, back_recv, home_send, home_recv,
+    load, local, back_local, z_send, z_recv, xy_send, xy_recv, back_send, back_recv, home_send, home_recv,
     p_send, p_recv, t_send, t_recv,
 ):
     g, j = lax.axis_index("gz"), lax.axis_index("gy")
@@ -247,7 +271,17 @@
     loads = [
         pltpu.make_async_copy(volume.at[pl.ds(8 * i, 8)], planes.at[pl.ds(8 * i, 8)], load.at[i]) for i in range(5)
     ]
-    for item in loads:
+    smalls = (
+        (x_offs_in, x_offs),
+        (x_fracs_in, x_fracs),
+        (y_offs_in, y_offs),
+        (y_fracs_in, y_fracs),
+        (z_off_in, z_off),
+        (z_frac_in, z_frac),
+        (slopes_in, slopes),
+    )
+    smalls = [pltpu.make_async_copy(src, dst, load.at[5 + i]) for i, (src, dst) in enumerate(smalls)]
+    for item in smalls + loads:
         item.start()
     loop(1, PLACES, lambda d: signal(*at_z((w + d) % PLACES)))
     for c in range(2):
@@ -259,6 +293,8 @@
     own_home = is_self(p % 4, home_j)
     pl.when(jnp.logical_not(own_home))(lambda: signal(p % 4, home_j))
 
+    for item in smalls:
+        item.wait()
     params[...] = jnp.zeros((8, 128), F32)
     params[0:1, 0:32] = y_offs[...].astype(F32)
     params[1:2, 0:32] = y_fracs[...]
@@ -309,59 +345,73 @@
         z_owns[h].start()
     z_own.wait()
     loop(1, 4, lambda d: z_param_in(d).wait_recv())
-
-    def xy_out(h, d):
+    prepare_z(z_params, z_highs, z_lows, z_taps)
+    pl.when(jnp.logical_not(own_home))(lambda: y_in.wait_recv())
+    pl.when(mine)(lambda: y_own.wait())
+    prepare_y(y_params, y_highs, y_lows, y_taps)
+
+    def xy_out(k, h, d):
         t = (p + d) % PLACES
-        dst = block(columns, 2 * p + core)
-        return copy_to(block(outgoing, 16 * h + t), dst, xy_send.at[h, d], xy_recv.at[2 * p + core], *at_xy(t, h))
-
-    def xy_in(c, d):
+        dst = part_of(columns, 2 * p + core, k)
+        src = part_of(outgoing, 16 * h + t, k)
+        return copy_to(src, dst, xy_send.at[k, h, d], xy_recv.at[k, 2 * p + core], *at_xy(t, h))
+
+    def xy_in(k, c, d):
         s = (p + PLACES - d) % PLACES
-        src = block(outgoing, 16 * core + s)
-        return copy_to(src, block(columns, 2 * s + c), xy_send.at[0, d], xy_recv.at[2 * s + c], *at_xy(s, c))
+        src = part_of(outgoing, 16 * core + s, k)
+        dst = part_of(columns, 2 * s + c, k)
+        return copy_to(src, dst, xy_send.at[k, 0, d], xy_recv.at[k, 2 * s + c], *at_xy(s, c))
 
     xy_own = pltpu.make_async_copy(block(outgoing, 16 * core + p), block(columns, 2 * p + core), local.at[4])
 
     def middle(h):
         z_owns[h].wait()
         loop(1, PLACES, lambda d: z_in(h, d).wait_recv())
-        shear_z(h, gathered, z_params, outgoing, z_taps, mixed)
-        loop(1, PLACES, lambda d: xy_out(h, d).start())
-        pl.when(core != h)(lambda: xy_out(h, 0).start())
+        shear_z(h, gathered, z_highs, z_lows, outgoing, mixed)
+        for k in range(2):
+            loop(1, PLACES, lambda d: xy_out(k, h, d).start())
+            pl.when(core != h)(lambda: xy_out(k, h, 0).start())
         pl.when(core == h)(lambda: xy_own.start())
 
-    def back_out(c, d):
+    def back_out(k, c, d):
         t = (p + d) % PLACES
-        dst = block(returned, 16 * core + p)
-        return copy_to(block(returning, 2 * t + c), dst, back_send.at[c, d], back_recv.at[core, p], *at_xy(t, c))
-
-    def back_in(h, d):
+        src = part_of(returning, 2 * t + c, k)
+        dst = part_of(returned, 16 * core + p, k)
+        return copy_to(src, dst, back_send.at[k, c, d], back_recv.at[k, core, p], *at_xy(t, c))
+
+    def back_in(k, h, d):
         s = (p + PLACES - d) % PLACES
-        src = block(returning, 2 * s + core)
-        return copy_to(src, block(returned, 16 * h + s), back_send.at[0, d], back_recv.at[h, s], *at_xy(s, h))
-
-    back_own = pltpu.make_async_copy(block(returning, 2 * p + core), block(returned, 16 * core + p), local.at[5])
+        src = part_of(returning, 2 * s + core, k)
+        dst = part_of(returned, 16 * h + s, k)
+        return copy_to(src, dst, back_send.at[k, 0, d], back_recv.at[k, h, s], *at_xy(s, h))
+
+    back_owns = [
+        pltpu.make_async_copy(
+            part_of(returning, 2 * p + core, k), part_of(returned, 16 * core + p, k), back_local.at[k]
+        )
+        for k in range(2)
+    ]
 
     def columns_here():
-        for c in range(2):
-            loop(1, PLACES, lambda d: xy_in(c, d).wait_recv())
-        xy_in(1 - core, 0).wait_recv()
         xy_own.wait()
-        shear_y(columns, y_params, returning, y_taps, before, after)
-        for c in range(2):
-            loop(1, PLACES, lambda d: back_out(c, d).start())
-        back_out(1 - core, 0).start()
-        back_own.start()
-
-    def home_out(h, d):
-        t = (w + d) % PLACES
+        for k in range(2):
+            for c in range(2):
+                loop(1, PLACES, lambda d: xy_in(k, c, d).wait_recv())
+            xy_in(k, 1 - core, 0).wait_recv()
+            shear_y(k, columns, y_highs, y_lows, returning, before, after)
+            for c in range(2):
+                loop(1, PLACES, lambda d: back_out(k, c, d).start())
+            back_out(k, 1 - core, 0).start()
+            back_owns[k].start()
+
+    def home_out(h, t):
         src = block(rows, 16 * h + 4 * (t % 4) + t // 4)
-        return copy_to(src, block(landed, 16 * h + w), home_send.at[h, d], home_recv.at[h, w], *at_z(t))
+        return copy_to(src, block(landed, 16 * h + w), home_send.at[h, t], home_recv.at[h, w], *at_z(t))
 
     def home_in(h, d):
         s = (w + PLACES - d) % PLACES
         src = block(rows, 16 * h + 4 * (s % 4) + s // 4)
-        return copy_to(src, block(landed, 16 * h + s), home_send.at[h, d], home_recv.at[h, s], *at_z(s))
+        return copy_to(src, block(landed, 16 * h + s), home_send.at[h, s], home_recv.at[h, s], *at_z(s))
 
     home_owns = [
         pltpu.make_async_copy(block(rows, 16 * h + 4 * n + g), block(landed, 16 * h + w), local.at[6 + h])
@@ -369,16 +419,20 @@
     ]
 
     def finish(h):
-        loop(1, PLACES, lambda d: back_in(h, d).wait_recv())
-        pl.when(core != h)(lambda: back_in(h, 0).wait_recv())
-        pl.when(core == h)(lambda: back_own.wait())
-        turn_back(h, returned, rows, mixed)
-        loop(1, PLACES, lambda d: home_out(h, d).start())
+        for k in range(2):
+            loop(1, PLACES, lambda d: back_in(k, h, d).wait_recv())
+            pl.when(core != h)(lambda: back_in(k, h, 0).wait_recv())
+            pl.when(core == h)(lambda: back_owns[k].wait())
+            turn_back(h, k, returned, rows, mixed)
+
+            def send(d):
+                t = 8 * k + (w + d) % 8
+                pl.when(t != w)(lambda: home_out(h, t).start())
+
+            loop(0, 8, send)
         home_owns[h].start()
 
     middle(0)
-    pl.when(jnp.logical_not(own_home))(lambda: y_in.wait_recv())
-    pl.when(mine)(lambda: y_own.wait())
     pl.when(core == 0)(columns_here)
     middle(1)
     finish(0)
@@ -408,16 +462,18 @@
     pl.when(jnp.logical_not(mine))(lambda: y_out.wait_send())
     for h in range(2):
         loop(1, PLACES, lambda d: z_out(h, d).wait_send())
-        loop(1, PLACES, lambda d: xy_out(h, d).wait_send())
-        pl.when(core != h)(lambda h=h: xy_out(h, 0).wait_send())
-        loop(1, PLACES, lambda d: back_out(h, d).wait_send())
-    back_out(1 - core, 0).wait_send()
+        for k in range(2):
+            loop(1, PLACES, lambda d: xy_out(k, h, d).wait_send())
+            pl.when(core != h)(lambda h=h, k=k: xy_out(k, h, 0).wait_send())
+            loop(1, PLACES, lambda d: back_out(k, h, d).wait_send())
+    for k in range(2):
+        back_out(k, 1 - core, 0).wait_send()
     pl.when(home_j == j)(lambda: term_own().wait())
     for b in range(4):
         pl.when(jnp.logical_not(is_self(b, home_j)))(lambda b=b: term_out(b).wait_send())
         pl.when(jnp.logical_not(is_self(owner_g, owner_j(b))))(lambda b=b: term_in(b).wait_recv())
     for h in range(2):
-        loop(1, PLACES, lambda d: home_out(h, d).wait_send())
+        loop(1, PLACES, lambda d: home_out(h, (w + d) % PLACES).wait_send())
         home_owns[h].wait()
         loop(1, PLACES, lambda d: home_in(h, d).wait_recv())
 
@@ -428,11 +484,10 @@
     many = lambda *shape: pltpu.SemaphoreType.DMA(shape)
     smem = pltpu.SMEM
     whole = ROWS * PLANES
-    spaces = (smem, smem, smem, smem, smem, pltpu.VMEM, pltpu.VMEM, pl.ANY)
     landed, projections = pl.pallas_call(
         rotate,
         out_shape=(array(whole, 128), array(2, 4, 8, 128)),
-        in_specs=[pl.BlockSpec(memory_space=space) for space in spaces],
+        in_specs=[pl.BlockSpec(memory_space=pltpu.HBM)] * 8,
         out_specs=[pl.BlockSpec(memory_space=pl.ANY)] * 2,
         scratch_shapes=[
             vmem(PLANES, ROWS, 128),
@@ -440,6 +495,15 @@
             vmem(whole, 128),
             vmem(whole // 2, 128),
             *[vmem(whole, 128)] * 7,
+            smem((DEPTH,), jnp.int32),
+            smem((DEPTH,), F32),
+            smem((1,), jnp.int32),
+            smem((1,), F32),
+            smem((TILTS,), jnp.int32),
+            pltpu.VMEM((1, 32), jnp.int32),
+            vmem(1, 32),
+            *[pltpu.VMEM((8, DEPTH // 2, DEPTH), BF16)] * 2,
+            *[pltpu.VMEM((8, 128, 128), BF16)] * 2,
             vmem(8, 128),
             vmem(4, 8, 128),
             vmem(8, 128),
@@ -448,14 +512,15 @@
             vmem(8, 256),
             vmem(2 * SLOPE + 1, 8, 128),
             vmem(TILTS, 8, 128),
-            many(5),
+            many(12),
             many(8),
+            many(2),
             many(2, PLACES),
             many(2, PLACES),
-            many(2, PLACES),
-            many(2 * PLACES),
-            many(2, PLACES),
-            many(2, PLACES),
+            many(2, 2, PLACES),
+            many(2, 2 * PLACES),
+            many(2, 2, PLACES),
+            many(2, 2, PLACES),
             many(2, PLACES),
             many(2, PLACES),
             many(5),
@@ -464,7 +529,7 @@
             many(4),
         ],
         compiler_params=pltpu.CompilerParams(
-            vmem_limit_bytes=VMEM_BYTES, collective_id=0, has_side_effects=True
+            vmem_limit_bytes=ALL_VMEM_BYTES, collective_id=0, has_side_effects=True
         ),
     )(
         x_offsets,
@@ -476,12 +541,20 @@
         y_fracs.reshape(1, 32),
         volume.reshape(PLANES, ROWS, 128),
     )
-    rotated = pl.pallas_call(
+    rotated, projections = pl.pallas_call(
         restore,
-        out_shape=array(PLANES, ROWS, 128),
-        in_specs=[pl.BlockSpec(memory_space=pltpu.VMEM)],
-        compiler_params=pltpu.CompilerParams(vmem_limit_bytes=VMEM_BYTES),
-    )(landed)
+        grid=(PLANES // 8,),
+        out_shape=(array(PLANES, ROWS, 128), array(2, 4, 8, 128)),
+        in_specs=[
+            pl.BlockSpec((ROWS, 8, 128), lambda i: (0, i, 0)),
+            pl.BlockSpec((2, 4, 8, 128), lambda i: (0, 0, 0, 0)),
+        ],
+        out_specs=[
+            pl.BlockSpec((8, ROWS, 128), lambda i: (i, 0, 0)),
+            pl.BlockSpec((2, 4, 8, 128), lambda i: (0, 0, 0, 0)),
+        ],
+        compiler_params=pltpu.CompilerParams(vmem_limit_bytes=ALL_VMEM_BYTES),
+    )(landed.reshape(ROWS, PLANES, 128), projections)
     return rotated.reshape(PLANES, 1, ROWS * 128), projections.reshape(2, 32, 128)
 
 

time: 103 us -> 103 us (level)
  the two profiles are of different devices: /device:TPU:41 before, /device:TPU:25 now
where the time goes in v3:
time: 103 us
  Pallas kernels  101 us (98%)
  between operations  1.93 us (2%)
    pallas_call x1, Pallas kernels, local(): pl.pallas_call(rotate, out_shape=(array(whole, 128), array(2, 4, 8, 128))...  97.1 us
    pallas_call x1, Pallas kernels, local(): pl.pallas_call(restore, grid=(PLANES // 8,), out_shape=(array(PLANES, ROW...  3.8 us

profile of v3, /device:TPU:25, one launch (start us, length us, event | category | flops | bytes accessed | tf_op | source)
XLA Modules:
  0.0 102.8 jit_solution(10528243043107816388)
XLA Ops:
  1.9 97.1 %shard_map.95 = (f32[1280,128]{1,0:T(8,128)}, f32[2,4,8,128]{3,2,1,0:T(8,128)}) custom-call(s32[160]{0:T(256)} %x_offs_in.1, f32[160]{0:T(256)} %x_fracs_in.1, s32[1]{0:T(128)S(6)} %copy.11.z_off_in, f32[1]{0:T(128)S(6)} %copy.12.z_frac_in, s32[8]{0:T(128)} %slopes_in.1, s32[1,32]{1,0:T(1,128)} %bitcast.8, f32[1,32]{1,0:T(1,128)} %bitcast.9, ...), custom_call_target="tpu_custom_call" | custom-call | tf_op jit(solution)/shard_map/pallas_call | solution.py:487
  99.0 3.8 %shard_map.96 = (f32[40,32,128]{2,1,0:T(8,128)}, f32[2,4,8,128]{3,2,1,0:T(8,128)}) custom-call(f32[32,40,128]{2,1,0:T(8,128)} %bitcast.7, f32[2,4,8,128]{3,2,1,0:T(8,128)} %get-tuple-element.7.terms), custom_call_target="tpu_custom_call" | custom-call | tf_op jit(solution)/shard_map/pallas_call | solution.py:544

commit v4 on v3

--- a/solution.py
+++ b/solution.py
@@ -55,6 +55,10 @@
 
 def block(ref, index):
     return ref.at[pl.ds(pl.multiple_of(PLANES * index, 8), PLANES)]
+
+
+def far_first(i):
+    return 8 + (i + 1) // 2 * (1 - 2 * (i % 2))
 
 
 def part_of(ref, index, k):
@@ -87,8 +91,10 @@
     row = iota((ROWS, 128), 0)
 
     def plane(z, carry):
-        matrix = band(taps[pl.ds(z, 1), :], 128)
-        total = product(halves(planes[z]), halves(matrix))
+        matrix_high, matrix_low = halves(band(taps[pl.ds(z, 1), :], 128))
+        high, low = halves(planes[z])
+        both = jnp.dot(jnp.concatenate([high, low], axis=0), matrix_high, preferred_element_type=F32)
+        total = both[:ROWS] + (both[ROWS:] + jnp.dot(high, matrix_low, preferred_element_type=F32))
         after = jnp.where(row < ROWS - 1, pltpu.roll(total[:, :128], ROWS - 1, 0), 0.0)
         before = jnp.where(row > 0, pltpu.roll(total[:, 256:], 1, 0), 0.0)
         out[pl.ds(z, ROWS, stride=PLANES), :] = total[:, 128:256] + (after + before)
@@ -212,9 +218,8 @@
 
 
 def restore(lines, terms, out, projections):
-    for z in range(8):
-        for part in range(ROWS // 8):
-            out[z, 8 * part : 8 * part + 8, :] = lines[8 * part : 8 * part + 8, z, :]
+    for z in range(PLANES):
+        out[z] = lines[pl.ds(z, ROWS, stride=PLANES), :]
     projections[...] = terms[...]
 
 
@@ -341,7 +346,8 @@
         for h in range(2)
     ]
     for h in range(2):
-        loop(1, PLACES, lambda d: z_out(h, d).start())
+        loop(0, PLACES - 1, lambda i: z_out(h, far_first(i)).start())
+    for h in range(2):
         z_owns[h].start()
     z_own.wait()
     loop(1, 4, lambda d: z_param_in(d).wait_recv())
@@ -425,11 +431,11 @@
             pl.when(core == h)(lambda: back_owns[k].wait())
             turn_back(h, k, returned, rows, mixed)
 
-            def send(d):
-                t = 8 * k + (w + d) % 8
-                pl.when(t != w)(lambda: home_out(h, t).start())
-
-            loop(0, 8, send)
+            def send(i):
+                t = (w + far_first(i)) % PLACES
+                pl.when(t // 8 == k)(lambda: home_out(h, t).start())
+
+            loop(0, PLACES - 1, send)
         home_owns[h].start()
 
     middle(0)
@@ -543,18 +549,10 @@
     )
     rotated, projections = pl.pallas_call(
         restore,
-        grid=(PLANES // 8,),
         out_shape=(array(PLANES, ROWS, 128), array(2, 4, 8, 128)),
-        in_specs=[
-            pl.BlockSpec((ROWS, 8, 128), lambda i: (0, i, 0)),
-            pl.BlockSpec((2, 4, 8, 128), lambda i: (0, 0, 0, 0)),
-        ],
-        out_specs=[
-            pl.BlockSpec((8, ROWS, 128), lambda i: (i, 0, 0)),
-            pl.BlockSpec((2, 4, 8, 128), lambda i: (0, 0, 0, 0)),
-        ],
-        compiler_params=pltpu.CompilerParams(vmem_limit_bytes=ALL_VMEM_BYTES),
-    )(landed.reshape(ROWS, PLANES, 128), projections)
+        in_specs=[pl.BlockSpec(memory_space=pltpu.VMEM)] * 2,
+        compiler_params=pltpu.CompilerParams(vmem_limit_bytes=VMEM_BYTES),
+    )(landed, projections)
     return rotated.reshape(PLANES, 1, ROWS * 128), projections.reshape(2, 32, 128)
 
 

time: 103 us -> 101 us (0.981)
  Pallas kernels: 101 us -> 97.1 us
  local copies, waits for them, and re-layouts: 0 us -> 1.84 us
    pallas_call x1, Pallas kernels: 3.8 us -> 0.96 us  [local(): pl.pallas_call(restore, out_shape=(array(PLANES, ROWS, 128), array(2, 4,...]
    unnamed x0 -> x4, local copies, waits for them, and re-layouts: none -> 1.84 us
where the time goes in v4:
time: 101 us
  Pallas kernels  97.1 us (96%)
  between operations  1.94 us (2%)
  local copies, waits for them, and re-layouts  1.84 us (2%)
    pallas_call x1, Pallas kernels, local(): pl.pallas_call(rotate, out_shape=(array(whole, 128), array(2, 4, 8, 128))...  96.1 us

profile of v4, /device:TPU:25, one launch (start us, length us, event | category | flops | bytes accessed | tf_op | source)
XLA Modules:
  0.0 100.8 jit_solution(5724147579387322409)
XLA Ops:
  1.9 96.1 %shard_map.95 = (f32[1280,128]{1,0:T(8,128)}, f32[2,4,8,128]{3,2,1,0:T(8,128)}) custom-call(s32[160]{0:T(256)} %x_offs_in.1, f32[160]{0:T(256)} %x_fracs_in.1, s32[1]{0:T(128)S(6)} %copy.11.z_off_in, f32[1]{0:T(128)S(6)} %copy.12.z_frac_in, s32[8]{0:T(128)} %slopes_in.1, s32[1,32]{1,0:T(1,128)} %bitcast.6, f32[1,32]{1,0:T(1,128)} %bitcast.7, ...), custom_call_target="tpu_custom_call" | custom-call | tf_op jit(solution)/shard_map/pallas_call | solution.py:493
  98.0 0.0 copy-start
  98.1 1.1 %copy-done = f32[1280,128]{1,0:T(8,128)S(1)} copy-done((f32[1280,128]{1,0:T(8,128)S(1)}, f32[1280,128]{1,0:T(8,128)}, u32[]{:S(2)}) %copy-start) | copy-done | bytes 655384
  99.1 0.0 copy-start.1
  99.1 0.8 copy-done.1
  99.9 1.0 shard_map.96
Async XLA Ops:
  98.0 1.1 %copy-start = (f32[1280,128]{1,0:T(8,128)S(1)}, f32[1280,128]{1,0:T(8,128)}, u32[]{:S(2)}) copy-start(f32[1280,128]{1,0:T(8,128)} %get-tuple-element.6.lines) | copy-start | bytes 1966084
  99.1 0.8 copy-start.1

commit v5 on v4

--- a/solution.py
+++ b/solution.py
@@ -59,6 +59,9 @@
 
 def far_first(i):
     return 8 + (i + 1) // 2 * (1 - 2 * (i % 2))
+
+
+PLANE_STEPS = (10, 6, 9, 11, 14, 2, 8, 5, 7, 13, 15, 4, 12, 1, 3)
 
 
 def part_of(ref, index, k):
@@ -101,7 +104,7 @@
         return carry
 
     arrive()
-    lax.fori_loop(0, PLANES, plane, 0, unroll=4)
+    lax.fori_loop(0, PLANES, plane, 0, unroll=10)
 
 
 def prepare_z(params, highs, lows, taps):
@@ -375,7 +378,8 @@
         loop(1, PLACES, lambda d: z_in(h, d).wait_recv())
         shear_z(h, gathered, z_highs, z_lows, outgoing, mixed)
         for k in range(2):
-            loop(1, PLACES, lambda d: xy_out(k, h, d).start())
+            for d in PLANE_STEPS:
+                xy_out(k, h, d).start()
             pl.when(core != h)(lambda: xy_out(k, h, 0).start())
         pl.when(core == h)(lambda: xy_own.start())
 
@@ -405,8 +409,9 @@
                 loop(1, PLACES, lambda d: xy_in(k, c, d).wait_recv())
             xy_in(k, 1 - core, 0).wait_recv()
             shear_y(k, columns, y_highs, y_lows, returning, before, after)
-            for c in range(2):
-                loop(1, PLACES, lambda d: back_out(k, c, d).start())
+            for d in PLANE_STEPS:
+                for c in range(2):
+                    back_out(k, c, d).start()
             back_out(k, 1 - core, 0).start()
             back_owns[k].start()
 

time: 101 us -> 99.5 us (0.985); the launches traced: 101 us -> 98.2 us
  Pallas kernels: 97.1 us -> 94.4 us
    pallas_call x1, Pallas kernels: 96.1 us -> 93.5 us  [local(): pl.pallas_call(rotate, out_shape=(array(whole, 128), array(2, 4, 8, 128))...]
where the time goes in v5:
time: 99.5 us; the launch traced here: 98.2 us
  Pallas kernels  94.4 us (95%)
  between operations  1.94 us (2%)
  local copies, waits for them, and re-layouts  1.84 us (2%)
    pallas_call x1, Pallas kernels, local(): pl.pallas_call(rotate, out_shape=(array(whole, 128), array(2, 4, 8, 128))...  93.5 us

profile of v5, /device:TPU:25, one launch (start us, length us, event | category | flops | bytes accessed | tf_op | source)
XLA Modules:
  0.0 98.2 jit_solution(13046084671636967885)
XLA Ops:
  1.9 93.5 %shard_map.95 = (f32[1280,128]{1,0:T(8,128)}, f32[2,4,8,128]{3,2,1,0:T(8,128)}) custom-call(s32[160]{0:T(256)} %x_offs_in.1, f32[160]{0:T(256)} %x_fracs_in.1, s32[1]{0:T(128)S(6)} %copy.11.z_off_in, f32[1]{0:T(128)S(6)} %copy.12.z_frac_in, s32[8]{0:T(128)} %slopes_in.1, s32[1,32]{1,0:T(1,128)} %bitcast.6, f32[1,32]{1,0:T(1,128)} %bitcast.7, ...), custom_call_target="tpu_custom_call" | custom-call | tf_op jit(solution)/shard_map/pallas_call | solution.py:498
  95.4 0.0 copy-start
  95.4 1.1 %copy-done = f32[1280,128]{1,0:T(8,128)S(1)} copy-done((f32[1280,128]{1,0:T(8,128)S(1)}, f32[1280,128]{1,0:T(8,128)}, u32[]{:S(2)}) %copy-start) | copy-done | bytes 655384
  96.5 0.0 copy-start.1
  96.5 0.8 copy-done.1
  97.3 1.0 shard_map.96
Async XLA Ops:
  95.4 1.1 %copy-start = (f32[1280,128]{1,0:T(8,128)S(1)}, f32[1280,128]{1,0:T(8,128)}, u32[]{:S(2)}) copy-start(f32[1280,128]{1,0:T(8,128)} %get-tuple-element.6.lines) | copy-start | bytes 1966084
  96.5 0.8 copy-start.1
